TPU v7x, 32 devices: a whole 2x2x4 slice. The times are simulated.
32 devices in a mesh: mode: 2 (over x), space: 16 (over z, y, core).
Axes of the slice: x: 2, y: 2, z: 4, core: 2. Of those that a mesh axis runs over, the one named last changes fastest.
Arguments:
- field: bfloat16 [64, 256, 1024], P('mode', 'space'), may hold values from -6 to 6
- kappa_x: float32 [8, 256, 1024], P(None, 'space'), may hold values from -4 to 4
- kappa_y: float32 [8, 256, 1024], P(None, 'space'), may hold values from -4 to 4
- coupling: bfloat16 [4, 8, 32, 32], P('mode'), may hold values from -0.625 to 0.625
- pattern: int32 [4, 8, 32, 32], P('mode'), may hold values 0 or 1
Outputs:
- image: float32 [64, 256, 1024], P('mode', 'space')
All inputs are finite; a program needn't handle non-finite values. No bound on the sum of `pattern` on one device may be relied on, other than what follows from the above.
Results may differ from a plain program's by a relative error of at most 0.0003.
Values may be sent and summed in bfloat16 or wider, within the bound.
A program may use at most 64 MiB of HBM per device.

v0:
```python
import functools

import jax
import jax.numpy as jnp
from jax import lax
from jax.experimental import pallas as pl
from jax.experimental.pallas import tpu as pltpu
from jax.sharding import PartitionSpec as P

LANES = 512


def kernel(n_mode, n_space, field_hbm, kx_hbm, ky_hbm, coup_hbm, pat_hbm, out_ref,
           raw, tall, u_ext, v_ext, kx_ref, ky_ref, coup, pat, packed, packed_in, pair_ref,
           kx_in, fx_prev, fy_row, held, last_row, sh,
           local_sem, main_send, main_recv, halo_send, halo_recv):
    mb, rows, ny = field_hbm.shape
    group = 128 // mb
    terms = kx_hbm.shape[0]
    sides = v_ext.shape[0]
    mode = lax.axis_index("mode")
    space = lax.axis_index("space")
    above = {"space": lax.rem(space + 1, n_space)}
    below = {"space": lax.rem(space + n_space - 1, n_space)}
    upper = {"mode": lax.rem(mode + 1, n_mode)}
    lower = {"mode": lax.rem(mode + n_mode - 1, n_mode)}

    barrier = pltpu.get_barrier_semaphore()
    for target in (above, below, upper, lower):
        pl.semaphore_signal(barrier, inc=1, device_id=target, device_id_type=pl.DeviceIdType.MESH)
    locals_ = [
        pltpu.make_async_copy(src, dst, local_sem.at[i])
        for i, (src, dst) in enumerate([
            (field_hbm.at[:, pl.ds(0, 8), :], raw.at[:, pl.ds(0, 8), :]),
            (field_hbm.at[:, pl.ds(8, rows - 8), :], raw.at[:, pl.ds(8, rows - 8), :]),
            (coup_hbm, coup), (pat_hbm, pat), (kx_hbm, kx_ref), (ky_hbm, ky_ref)])]
    for copy in locals_:
        copy.start()

    def masked(slot, k):
        return jnp.where(pat[slot, k] > 0, coup[slot, k].astype(jnp.float32), 0.0)

    def placed(block, shape, offset, flip=False):
        spot = lax.broadcasted_iota(jnp.int32, shape, 0) + offset
        place = jnp.where(lax.broadcasted_iota(jnp.int32, shape, 1) == spot, 1.0, 0.0).astype(jnp.bfloat16)
        return lax.dot_general(block.astype(jnp.bfloat16), place, (((0 if flip else 1,), (0,)), ((), ())),
                               preferred_element_type=jnp.float32)

    def by_rows(first, count):
        for c in range(0, ny, 128):
            tall[:mb * count] = raw[:, first:first + count, c:c + 128].astype(jnp.float32).reshape(mb * count, 128)
            for r in range(count):
                u_ext[first + r + 1, :, c:c + 128] = tall[pl.ds(r, mb, stride=count), :].astype(jnp.bfloat16)

    locals_[0].wait()
    by_rows(0, 8)
    pl.semaphore_wait(barrier, 4)

    def remote(src, dst, send, recv, target):
        return pltpu.make_async_remote_copy(
            src_ref=src, dst_ref=dst, send_sem=send, recv_sem=recv,
            device_id=target, device_id_type=pl.DeviceIdType.MESH)

    towards = (lower, upper)

    def row_copy(side, r):
        return remote(u_ext.at[r + 1], v_ext.at[side, r + 1], main_send.at[side, r], main_recv.at[side, r], towards[side])

    def halo_up(side):
        return remote(v_ext.at[side, rows], v_ext.at[side, 0], halo_send.at[4 + side], halo_recv.at[4 + side], above)

    def halo_down(side):
        return remote(v_ext.at[side, 1], v_ext.at[side, rows + 1], halo_send.at[6 + side], halo_recv.at[6 + side], below)

    coup_copy = remote(packed, packed_in, halo_send.at[0], halo_recv.at[0], upper)
    last_copy = remote(u_ext.at[rows], u_ext.at[0], halo_send.at[1], halo_recv.at[1], above)
    first_copy = remote(u_ext.at[1], u_ext.at[rows + 1], halo_send.at[2], halo_recv.at[2], below)
    kx_copy = remote(kx_hbm.at[:, pl.ds(rows - 8, 8), :], kx_in, halo_send.at[3], halo_recv.at[3], above)

    for side in range(sides):
        row_copy(side, 0).start()
    first_copy.start()
    kx_copy.start()
    locals_[1].wait()
    by_rows(8, rows - 8)
    for side in range(sides):
        row_copy(side, rows - 1).start()
        row_copy(side, 1).start()
        row_copy(side, 2).start()
    last_copy.start()

    locals_[2].wait()
    locals_[3].wait()
    for q in range(terms // group):
        beside = None
        for p in range(group):
            part = placed(masked(1, q * group + p), (mb, 128), p * mb, flip=True)
            beside = part if beside is None else beside + part
        packed[q * mb:(q + 1) * mb] = beside.astype(jnp.bfloat16)

    coup_copy.start()
    for side in range(sides):
        @pl.loop(3, rows - 1)
        def _(r):
            row_copy(side, r).start()

    for side in range(sides):
        row_copy(side, 0).wait_recv()
        halo_down(side).start()
        row_copy(side, rows - 1).wait_recv()
        halo_up(side).start()
    coup_copy.wait_recv()
    for copy in locals_[4:]:
        copy.wait()

    for k in range(terms):
        q, p = divmod(k, group)
        half = masked(0, k) * 0.5
        shape = (mb, 4 * mb)
        coef = (placed(half, shape, 0) + placed(half, shape, mb, flip=True) + placed(masked(1, k), shape, 2 * mb)
                + placed(packed_in[q * mb:(q + 1) * mb, p * mb:(p + 1) * mb], shape, 3 * mb)).astype(jnp.bfloat16)
        pair_ref[k * mb:(k + 1) * mb, :4 * mb] = coef
        pair_ref[k * mb:(k + 1) * mb, 4 * mb:] = -coef

    last_copy.wait_recv()
    first_copy.wait_recv()
    kx_copy.wait_recv()
    for side in range(sides):
        halo_up(side).wait_recv()
        halo_down(side).wait_recv()

    @pl.when(space == n_space - 1)
    def _():
        u_ext[rows + 1] = jnp.zeros((mb, ny), jnp.bfloat16)
        for side in range(sides):
            v_ext[side, rows + 1] = jnp.zeros((mb, ny), jnp.bfloat16)

    pair = pair_ref[...]

    def stack(e, cols):
        u = u_ext[e, :, cols]
        vs = [v_ext[side, e, :, cols] for side in range(sides)]
        return [u, u, vs[0], vs[-1]]

    def weighted(diff, weight_of):
        total = None
        for k in range(terms):
            part = weight_of(k) * diff[k * mb:(k + 1) * mb]
            total = part if total is None else total + part
        return total

    def flux_x(e, cols, weight_of):
        diff = jnp.dot(pair, jnp.concatenate(stack(e + 1, cols) + stack(e, cols), axis=0),
                       preferred_element_type=jnp.float32)
        return weighted(diff, weight_of)

    blocks = [pl.ds(c, LANES) for c in range(0, ny, LANES)]
    keep = jnp.where(space == 0, 0.0, 1.0).astype(jnp.float32)
    for cols in blocks:
        fx_prev[:, cols] = flux_x(0, cols, lambda k: kx_in[k, 7:8, cols]) * keep

    def shifted(x):
        lane = lax.broadcasted_iota(jnp.int32, x.shape, 1)
        moved = pltpu.roll(x.astype(jnp.float32), ny - 1, axis=1)
        return jnp.where(lane == ny - 1, 0.0, moved).astype(jnp.bfloat16)

    def kx_row(r, cols):
        return lambda k: kx_ref[k, pl.ds(r, 1), cols]

    def flux_y_part(r):
        e = r + 1
        sh[0] = shifted(u_ext[e])
        for side in range(sides):
            sh[1 + side] = shifted(v_ext[side, e])
        for cols in blocks:
            ahead = [sh[0, :, cols]] * 2 + [sh[1, :, cols], sh[sides, :, cols]]
            diff = jnp.dot(pair, jnp.concatenate(ahead + stack(e, cols), axis=0),
                           preferred_element_type=jnp.float32)
            fy_row[:, cols] = weighted(diff, lambda k: ky_ref[k, pl.ds(r, 1), cols])
        fy = fy_row[...]
        lane = lax.broadcasted_iota(jnp.int32, fy.shape, 1)
        return jnp.where(lane == 0, 0.0, pltpu.roll(fy, 1, axis=1)) - fy

    def put(r, cols, value):
        for at in range(0, LANES, 128):
            tile = (cols.start + at) // 128
            start = (r // 8) * 8 * (ny // 128) + tile * 8 + r % 8
            out_ref[pl.ds(start, mb, stride=rows * (ny // 128)), :] = value[:, at:at + 128]

    def flux_x_step(r):
        for cols in blocks:
            fx = flux_x(r + 1, cols, kx_row(r, cols))
            put(r, cols, fx_prev[:, cols] - fx + held[:, cols])
            fx_prev[:, cols] = fx

    final = rows - 1
    last_row[...] = flux_y_part(final)
    for cols in blocks:
        last_row[:, cols] = last_row[:, cols] - flux_x(rows, cols, kx_row(final, cols))

    @pl.loop(0, rows - 3)
    def _(r):
        held[...] = flux_y_part(r)
        for side in range(sides):
            row_copy(side, r + 1).wait_recv()
        flux_x_step(r)

    held[...] = flux_y_part(rows - 3)
    for side in range(sides):
        row_copy(side, rows - 2).wait_recv()
    flux_x_step(rows - 3)
    held[...] = flux_y_part(rows - 2)
    flux_x_step(rows - 2)
    for cols in blocks:
        put(final, cols, last_row[:, cols] + fx_prev[:, cols])

    for side in range(sides):
        @pl.loop(0, rows)
        def _(r):
            row_copy(side, r).wait_send()
        halo_up(side).wait_send()
        halo_down(side).wait_send()
    for copy in (coup_copy, last_copy, first_copy, kx_copy):
        copy.wait_send()


def shards(n_mode, n_space, field, kappa_x, kappa_y, coupling, pattern):
    mb, rows, ny = field.shape
    terms = kappa_x.shape[0]
    sides = 1 if n_mode == 2 else 2
    vmem = pl.BlockSpec(memory_space=pltpu.VMEM)
    hbm = pl.BlockSpec(memory_space=pltpu.HBM)
    out = pl.pallas_call(
        functools.partial(kernel, n_mode, n_space),
        out_shape=jax.ShapeDtypeStruct((mb * rows * ny // 128, 128), jnp.float32),
        in_specs=[hbm] * 5,
        out_specs=vmem,
        scratch_shapes=[
            pltpu.VMEM(field.shape, jnp.bfloat16),
            pltpu.VMEM((mb * rows, 128), jnp.float32),
            pltpu.VMEM((rows + 2, mb, ny), jnp.bfloat16),
            pltpu.VMEM((sides, rows + 2, mb, ny), jnp.bfloat16),
            pltpu.VMEM(kappa_x.shape, jnp.float32),
            pltpu.VMEM(kappa_y.shape, jnp.float32),
            pltpu.VMEM(coupling.shape, jnp.bfloat16),
            pltpu.VMEM(pattern.shape, jnp.int32),
            pltpu.VMEM((terms * mb * mb // 128, 128), jnp.bfloat16),
            pltpu.VMEM((terms * mb * mb // 128, 128), jnp.bfloat16),
            pltpu.VMEM((terms * mb, 8 * mb), jnp.bfloat16),
            pltpu.VMEM((terms, 8, ny), jnp.float32),
            pltpu.VMEM((mb, ny), jnp.float32),
            pltpu.VMEM((mb, ny), jnp.float32),
            pltpu.VMEM((mb, ny), jnp.float32),
            pltpu.VMEM((mb, ny), jnp.float32),
            pltpu.VMEM((1 + sides, mb, ny), jnp.bfloat16),
            pltpu.SemaphoreType.DMA((6,)),
            pltpu.SemaphoreType.DMA((sides, rows)),
            pltpu.SemaphoreType.DMA((sides, rows)),
            pltpu.SemaphoreType.DMA((9,)),
            pltpu.SemaphoreType.DMA((9,)),
        ],
        compiler_params=pltpu.CompilerParams(collective_id=0, has_side_effects=True, vmem_limit_bytes=24 * 2**20),
    )(*[pltpu.with_memory_space_constraint(x, pltpu.HBM)
        for x in (field, kappa_x, kappa_y, coupling, pattern)])
    tiles = out.reshape(mb, rows // 8, ny // 128, 8, 128)
    return jnp.swapaxes(tiles, 2, 3).reshape(mb, rows, ny)


def solution(mesh):
    placed = (
        P("mode", "space", None),
        P(None, "space", None),
        P(None, "space", None),
        P("mode", None, None, None),
        P("mode", None, None, None),
    )
    return jax.shard_map(
        functools.partial(shards, mesh.shape["mode"], mesh.shape["space"]),
        mesh=mesh, in_specs=placed, out_specs=P("mode", "space", None), check_vma=False)
```

profile of v0, /device:TPU:0, one launch (start us, length us, event | category | flops | bytes accessed | tf_op | source)
XLA Modules:
  0.0 31.5 jit_solution(11591549961627816773)
XLA Ops:
  0.0 30.1 %shard_map.55 = f32[4096,128]{1,0:T(8,128)S(1)} custom-call(bf16[32,16,1024]{2,1,0:T(8,128)(2,1)} %field_hbm.1, f32[8,16,1024]{2,1,0:T(8,128)} %kx_hbm.1, f32[8,16,1024]{2,1,0:T(8,128)} %ky_hbm.1, bf16[2,8,32,32]{3,2,1,0:T(8,128)(2,1)} %coup_hbm.1, s32[2,8,32,32]{3,2,1,0:T(8,128)} %pat_hbm.1), custom_call_target="tpu_custom_call" | custom-call | tf_op jit(solution)/shard_map/pallas_call | solution.py:233
  30.1 1.3 %copy.7 = f32[32,16,1024]{2,1,0:T(8,128)} copy(f32[32,16,1024]{2,1,0:T(8,128)S(1)} %bitcast.5) | data formatting | bytes 4194304
where the time goes:
time: 31.6 us; the launch traced here: 31.5 us
  Pallas kernels  30.1 us (95%)
  local copies, waits for them, and re-layouts  1.32 us (4%)
    pallas_call x1, Pallas kernels, shards(): pl.pallas_call(functools.partial(kernel, n_mode, n_space), out_shape=jax....  30.1 us
    unnamed x1, local copies, waits for them, and re-layouts  1.32 us

commit v1 on v0

--- a/solution.py
+++ b/solution.py
@@ -26,8 +26,16 @@
     lower = {"mode": lax.rem(mode + n_mode - 1, n_mode)}
 
     barrier = pltpu.get_barrier_semaphore()
-    for target in (above, below, upper, lower):
+    has_below = space > 0
+    has_above = space < n_space - 1
+
+    def greet(target):
         pl.semaphore_signal(barrier, inc=1, device_id=target, device_id_type=pl.DeviceIdType.MESH)
+
+    for target in (upper, lower)[:sides]:
+        greet(target)
+    pl.when(has_below)(lambda: greet(below))
+    pl.when(has_above)(lambda: greet(above))
     locals_ = [
         pltpu.make_async_copy(src, dst, local_sem.at[i])
         for i, (src, dst) in enumerate([
@@ -54,7 +62,7 @@
 
     locals_[0].wait()
     by_rows(0, 8)
-    pl.semaphore_wait(barrier, 4)
+    pl.semaphore_wait(barrier, sides + jnp.where(has_below, 1, 0) + jnp.where(has_above, 1, 0))
 
     def remote(src, dst, send, recv, target):
         return pltpu.make_async_remote_copy(
@@ -79,15 +87,15 @@
 
     for side in range(sides):
         row_copy(side, 0).start()
-    first_copy.start()
-    kx_copy.start()
+    pl.when(has_below)(first_copy.start)
+    pl.when(has_above)(kx_copy.start)
     locals_[1].wait()
     by_rows(8, rows - 8)
     for side in range(sides):
         row_copy(side, rows - 1).start()
         row_copy(side, 1).start()
         row_copy(side, 2).start()
-    last_copy.start()
+    pl.when(has_above)(last_copy.start)
 
     locals_[2].wait()
     locals_[3].wait()
@@ -106,9 +114,9 @@
 
     for side in range(sides):
         row_copy(side, 0).wait_recv()
-        halo_down(side).start()
+        pl.when(has_below)(halo_down(side).start)
         row_copy(side, rows - 1).wait_recv()
-        halo_up(side).start()
+        pl.when(has_above)(halo_up(side).start)
     coup_copy.wait_recv()
     for copy in locals_[4:]:
         copy.wait()
@@ -122,18 +130,32 @@
         pair_ref[k * mb:(k + 1) * mb, :4 * mb] = coef
         pair_ref[k * mb:(k + 1) * mb, 4 * mb:] = -coef
 
-    last_copy.wait_recv()
-    first_copy.wait_recv()
-    kx_copy.wait_recv()
-    for side in range(sides):
-        halo_up(side).wait_recv()
-        halo_down(side).wait_recv()
-
-    @pl.when(space == n_space - 1)
-    def _():
-        u_ext[rows + 1] = jnp.zeros((mb, ny), jnp.bfloat16)
-        for side in range(sides):
-            v_ext[side, rows + 1] = jnp.zeros((mb, ny), jnp.bfloat16)
+    @pl.when(has_below)
+    def _():
+        last_copy.wait_recv()
+        kx_copy.wait_recv()
+        for side in range(sides):
+            halo_up(side).wait_recv()
+
+    @pl.when(has_above)
+    def _():
+        first_copy.wait_recv()
+        for side in range(sides):
+            halo_down(side).wait_recv()
+
+    def blank(e):
+        u_ext[e] = jnp.zeros((mb, ny), jnp.bfloat16)
+        for side in range(sides):
+            v_ext[side, e] = jnp.zeros((mb, ny), jnp.bfloat16)
+
+    @pl.when(jnp.logical_not(has_below))
+    def _():
+        blank(0)
+        kx_in[...] = jnp.zeros_like(kx_in)
+
+    @pl.when(jnp.logical_not(has_above))
+    def _():
+        blank(rows + 1)
 
     pair = pair_ref[...]
 
@@ -155,9 +177,8 @@
         return weighted(diff, weight_of)
 
     blocks = [pl.ds(c, LANES) for c in range(0, ny, LANES)]
-    keep = jnp.where(space == 0, 0.0, 1.0).astype(jnp.float32)
     for cols in blocks:
-        fx_prev[:, cols] = flux_x(0, cols, lambda k: kx_in[k, 7:8, cols]) * keep
+        fx_prev[:, cols] = flux_x(0, cols, lambda k: kx_in[k, 7:8, cols])
 
     def shifted(x):
         lane = lax.broadcasted_iota(jnp.int32, x.shape, 1)
@@ -218,10 +239,17 @@
         @pl.loop(0, rows)
         def _(r):
             row_copy(side, r).wait_send()
-        halo_up(side).wait_send()
-        halo_down(side).wait_send()
-    for copy in (coup_copy, last_copy, first_copy, kx_copy):
-        copy.wait_send()
+    coup_copy.wait_send()
+
+    @pl.when(has_above)
+    def _():
+        for copy in (last_copy, kx_copy) + tuple(halo_up(side) for side in range(sides)):
+            copy.wait_send()
+
+    @pl.when(has_below)
+    def _():
+        for copy in (first_copy,) + tuple(halo_down(side) for side in range(sides)):
+            copy.wait_send()
 
 
 def shards(n_mode, n_space, field, kappa_x, kappa_y, coupling, pattern):

time: 31.6 us -> 31.2 us (0.987)
  Pallas kernels: 30.1 us -> 29.7 us
    pallas_call x1, Pallas kernels: 30.1 us -> 29.7 us  [shards(): pl.pallas_call(functools.partial(kernel, n_mode, n_space), out_shape=jax....]
where the time goes in v1:
time: 31.2 us; the launch traced here: 31 us
  Pallas kernels  29.7 us (95%)
  local copies, waits for them, and re-layouts  1.32 us (4%)
    pallas_call x1, Pallas kernels, shards(): pl.pallas_call(functools.partial(kernel, n_mode, n_space), out_shape=jax....  29.7 us
    unnamed x1, local copies, waits for them, and re-layouts  1.32 us

profile of v1, /device:TPU:0, one launch (start us, length us, event | category | flops | bytes accessed | tf_op | source)
XLA Modules:
  0.0 31.0 jit_solution(4867749122436722532)
XLA Ops:
  0.0 29.7 %shard_map.55 = f32[4096,128]{1,0:T(8,128)S(1)} custom-call(bf16[32,16,1024]{2,1,0:T(8,128)(2,1)} %field_hbm.1, f32[8,16,1024]{2,1,0:T(8,128)} %kx_hbm.1, f32[8,16,1024]{2,1,0:T(8,128)} %ky_hbm.1, bf16[2,8,32,32]{3,2,1,0:T(8,128)(2,1)} %coup_hbm.1, s32[2,8,32,32]{3,2,1,0:T(8,128)} %pat_hbm.1), custom_call_target="tpu_custom_call" | custom-call | tf_op jit(solution)/shard_map/pallas_call | solution.py:261
  29.7 1.3 %copy.7 = f32[32,16,1024]{2,1,0:T(8,128)} copy(f32[32,16,1024]{2,1,0:T(8,128)S(1)} %bitcast.5) | data formatting | bytes 4194304

commit v2 on v0

v2 whole, which is shorter than its diff:
```python
import functools

import jax
import jax.numpy as jnp
from jax import lax
from jax.experimental import pallas as pl
from jax.experimental.pallas import tpu as pltpu
from jax.sharding import PartitionSpec as P

LANES = 512
EARLY = 128
LATE = (384,)


def kernel(n_mode, n_space, field_hbm, kx_hbm, ky_hbm, coup_hbm, pat_hbm, out_ref,
           raw, raw_in, tall, u_ext, v_ext, kappa, coup, pat, packed, packed_in, pair_ref,
           kx_in, fx_prev, fy_row, held, first_row, last_row, ahead, sh,
           local_sem, field_send, early_recv, row_recv, piece_recv, other_send, other_recv):
    mb, rows, ny = field_hbm.shape
    group = 128 // mb
    terms = kx_hbm.shape[0]
    sides = v_ext.shape[0]
    early = raw_in.shape[-1]
    mode = lax.axis_index("mode")
    space = lax.axis_index("space")
    above = {"space": lax.rem(space + 1, n_space)}
    below = {"space": lax.rem(space + n_space - 1, n_space)}
    upper = {"mode": lax.rem(mode + 1, n_mode)}
    lower = {"mode": lax.rem(mode + n_mode - 1, n_mode)}
    has_below = space > 0
    has_above = space < n_space - 1
    kx_ref, ky_ref = kappa.at[0], kappa.at[1]

    barrier = pltpu.get_barrier_semaphore()

    def greet(target):
        pl.semaphore_signal(barrier, inc=1, device_id=target, device_id_type=pl.DeviceIdType.MESH)

    for target in (upper, lower)[:sides]:
        greet(target)
    pl.when(has_above)(lambda: greet(above))

    field_load = pltpu.make_async_copy(field_hbm, raw, local_sem.at[0])
    coup_load = pltpu.make_async_copy(coup_hbm, coup, local_sem.at[1])
    pat_load = pltpu.make_async_copy(pat_hbm, pat, local_sem.at[2])
    kx_load = pltpu.make_async_copy(kx_hbm, kx_ref, local_sem.at[3])
    ky_load = pltpu.make_async_copy(ky_hbm, ky_ref, local_sem.at[3])
    for copy in (field_load, coup_load, pat_load, kx_load, ky_load):
        copy.start()

    def masked(slot, k):
        return jnp.where(pat[slot, k] > 0, coup[slot, k].astype(jnp.float32), 0.0)

    def placed(block, shape, offset, flip=False):
        spot = lax.broadcasted_iota(jnp.int32, shape, 0) + offset
        place = jnp.where(lax.broadcasted_iota(jnp.int32, shape, 1) == spot, 1.0, 0.0).astype(jnp.bfloat16)
        return lax.dot_general(block.astype(jnp.bfloat16), place, (((0 if flip else 1,), (0,)), ((), ())),
                               preferred_element_type=jnp.float32)

    def by_rows(source, target, first, count, width):
        for c in range(0, width, 128):
            tall[:mb * count] = source[:, first:first + count, c:c + 128].astype(jnp.float32).reshape(mb * count, 128)
            for r in range(count):
                target[first + r + 1, :, c:c + 128] = tall[pl.ds(r, mb, stride=count), :].astype(jnp.bfloat16)

    pl.semaphore_wait(barrier, sides + jnp.where(has_below, 1, 0))

    def remote(src, dst, send, recv, target):
        return pltpu.make_async_remote_copy(
            src_ref=src, dst_ref=dst, send_sem=send, recv_sem=recv,
            device_id=target, device_id_type=pl.DeviceIdType.MESH)

    towards = (lower, upper)
    cuts = [early] + [ny - w for w in LATE if ny - w > early] + [ny]
    pieces = list(zip(cuts[:-1], cuts[1:]))
    pairs = (rows - 6) // 2
    rest = pl.ds(early, ny - early)

    def rows_copy(side, first, count, at, cols=rest, recv=row_recv):
        part = pl.ds(first + 1, count)
        return remote(u_ext.at[part, :, cols], v_ext.at[side, part, :, cols],
                      field_send.at[side], recv.at[side, at], towards[side])

    def pair_copy(side, h):
        return rows_copy(side, 2 * h + 2, 2, h + 2)

    def single_copy(side, r):
        return rows_copy(side, r, 1, r - (rows - 4) + pairs + 2)

    def piece_copy(side, p):
        first, last = pieces[p]
        return rows_copy(side, rows - 2, 1, p, pl.ds(first, last - first), piece_recv)

    def early_copy(side):
        return remote(field_hbm.at[:, :, pl.ds(0, early)], raw_in.at[side], field_send.at[side], early_recv.at[side], towards[side])

    def halo_up(side):
        return remote(v_ext.at[side, rows], v_ext.at[side, 0], other_send.at[1], other_recv.at[1], above)

    def halo_down(side):
        return remote(v_ext.at[side, 1], v_ext.at[side, rows + 1], other_send.at[2], other_recv.at[2], below)

    coup_copy = remote(packed, packed_in, other_send.at[0], other_recv.at[0], upper)
    last_copy = remote(u_ext.at[rows], u_ext.at[0], other_send.at[1], other_recv.at[1], above)
    first_copy = remote(u_ext.at[1], u_ext.at[rows + 1], other_send.at[2], other_recv.at[3], below)
    kx_copy = remote(kx_hbm.at[:, pl.ds(rows - 8, 8), :], kx_in, other_send.at[3], other_recv.at[4], above)

    def strips(count, sem):
        part = u_ext.at[pl.ds(0, count)]
        return pltpu.make_async_copy(part, part, sem)

    for side in range(sides):
        early_copy(side).start()

    coup_load.wait()
    pat_load.wait()
    for q in range(terms // group):
        beside = None
        for p in range(group):
            part = placed(masked(1, q * group + p), (mb, 128), p * mb, flip=True)
            beside = part if beside is None else beside + part
        packed[q * mb:(q + 1) * mb] = beside.astype(jnp.bfloat16)
    coup_copy.start()

    field_load.wait()
    by_rows(raw, u_ext, 0, rows, ny)
    for side in range(sides):
        rows_copy(side, 0, 2, 0).start()
        rows_copy(side, rows - 1, 1, 1).start()
    pl.when(has_below)(first_copy.start)
    for side in range(sides):
        @pl.loop(0, pairs)
        def _(h):
            pair_copy(side, h).start()
    for r in (rows - 4, rows - 3):
        for side in range(sides):
            single_copy(side, r).start()
    for p in range(len(pieces)):
        for side in range(sides):
            piece_copy(side, p).start()

    for k in range(terms):
        half = masked(0, k) * 0.5
        shape = (mb, 4 * mb)
        coef = placed(half, shape, 0) + placed(half, shape, mb, flip=True) + placed(masked(1, k), shape, 2 * mb)
        pair_ref[k * mb:(k + 1) * mb, :4 * mb] = coef.astype(jnp.bfloat16)

    @pl.when(has_above)
    def _():
        first_copy.wait_recv()
        last_copy.start()
        kx_copy.start()

    for side in range(sides):
        early_copy(side).wait_recv()
        by_rows(raw_in.at[side], v_ext.at[side], 0, rows, early)
    coup_copy.wait_recv()
    pltpu.make_async_copy(kappa, kappa, local_sem.at[3]).wait()
    for k in range(terms):
        q, p = divmod(k, group)
        shape = (mb, 4 * mb)
        coef = (pair_ref[k * mb:(k + 1) * mb, :4 * mb].astype(jnp.float32)
                + placed(packed_in[q * mb:(q + 1) * mb, p * mb:(p + 1) * mb], shape, 3 * mb)).astype(jnp.bfloat16)
        pair_ref[k * mb:(k + 1) * mb, :4 * mb] = coef
        pair_ref[k * mb:(k + 1) * mb, 4 * mb:] = -coef
    for side in range(sides):
        rows_copy(side, 0, 2, 0).wait_recv()
        pl.when(has_below)(halo_down(side).start)
        rows_copy(side, rows - 1, 1, 1).wait_recv()
        pl.when(has_above)(halo_up(side).start)

    pair = pair_ref[...]

    def stack(e, cols):
        u = u_ext[e, :, cols]
        vs = [v_ext[side, e, :, cols] for side in range(sides)]
        return [u, u, vs[0], vs[-1]]

    def weighted(diff, weight_of):
        total = None
        for k in range(terms):
            part = weight_of(k) * diff[k * mb:(k + 1) * mb]
            total = part if total is None else total + part
        return total

    def flux_x(e, cols, weight_of):
        diff = jnp.dot(pair, jnp.concatenate(stack(e + 1, cols) + stack(e, cols), axis=0),
                       preferred_element_type=jnp.float32)
        return weighted(diff, weight_of)

    blocks = [pl.ds(c, LANES) for c in range(0, ny, LANES)]

    def shifted(x):
        lane = lax.broadcasted_iota(jnp.int32, x.shape, 1)
        moved = pltpu.roll(x.astype(jnp.float32), ny - 1, axis=1)
        return jnp.where(lane == ny - 1, 0.0, moved).astype(jnp.bfloat16)

    def kx_row(r, cols):
        return lambda k: kx_ref[k, pl.ds(r, 1), cols]

    def flux_y_part(r):
        e = r + 1
        sh[0] = shifted(u_ext[e])
        for side in range(sides):
            sh[1 + side] = shifted(v_ext[side, e])
        for cols in blocks:
            next_cols = [sh[0, :, cols]] * 2 + [sh[1, :, cols], sh[sides, :, cols]]
            diff = jnp.dot(pair, jnp.concatenate(next_cols + stack(e, cols), axis=0),
                           preferred_element_type=jnp.float32)
            fy_row[:, cols] = weighted(diff, lambda k: ky_ref[k, pl.ds(r, 1), cols])
        fy = fy_row[...]
        lane = lax.broadcasted_iota(jnp.int32, fy.shape, 1)
        return jnp.where(lane == 0, 0.0, pltpu.roll(fy, 1, axis=1)) - fy

    def put(r, cols, value):
        for at in range(0, cols.size, 128):
            tile = (cols.start + at) // 128
            start = (r // 8) * 8 * (ny // 128) + tile * 8 + r % 8
            out_ref[pl.ds(start, mb, stride=rows * (ny // 128)), :] = value[:, at:at + 128]

    def flux_x_step(r):
        for cols in blocks:
            fx = flux_x(r + 1, cols, kx_row(r, cols))
            put(r, cols, fx_prev[:, cols] - fx + held[:, cols])
            fx_prev[:, cols] = fx

    final = rows - 1

    def edges():
        @pl.when(has_below)
        def _():
            strips(1 + sides, other_recv.at[1]).wait()
            kx_copy.wait_recv()

        @pl.when(has_above)
        def _():
            strips(sides, other_recv.at[2]).wait()

        def blank(e):
            u_ext[e] = jnp.zeros((mb, ny), jnp.bfloat16)
            for side in range(sides):
                v_ext[side, e] = jnp.zeros((mb, ny), jnp.bfloat16)

        @pl.when(jnp.logical_not(has_below))
        def _():
            blank(0)
            kx_in[...] = jnp.zeros_like(kx_in)

        @pl.when(jnp.logical_not(has_above))
        def _():
            blank(rows + 1)

        last_row[...] = flux_y_part(final)
        for cols in blocks:
            put(0, cols, first_row[:, cols] + flux_x(0, cols, lambda k: kx_in[k, 7:8, cols]))
            last_row[:, cols] = last_row[:, cols] - flux_x(rows, cols, kx_row(final, cols))

    first_row[...] = flux_y_part(0)
    for cols in blocks:
        fx = flux_x(1, cols, kx_row(0, cols))
        first_row[:, cols] = first_row[:, cols] - fx
        fx_prev[:, cols] = fx
    held[...] = flux_y_part(1)

    @pl.loop(0, pairs)
    def _(h):
        pl.when(h == pairs // 2)(edges)
        for side in range(sides):
            pair_copy(side, h).wait_recv()
        r = 2 * h + 1
        flux_x_step(r)
        held[...] = flux_y_part(r + 1)
        flux_x_step(r + 1)
        held[...] = flux_y_part(r + 2)

    @pl.loop(rows - 4, rows - 2)
    def _(r):
        for side in range(sides):
            single_copy(side, r).wait_recv()
        flux_x_step(r - 1)
        held[...] = flux_y_part(r)

    late = rows - 2

    def ahead_of(x, width):
        turned = pltpu.roll(x.astype(jnp.float32), x.shape[1] - 1, axis=1)
        if x.shape[1] == width:
            lane = lax.broadcasted_iota(jnp.int32, x.shape, 1)
            turned = jnp.where(lane == width - 1, 0.0, turned)
        return turned[:, :width].astype(jnp.bfloat16)

    for p, (first, last) in enumerate(pieces):
        first = 0 if p == 0 else first
        width = last - first
        cols = pl.ds(first, width)
        y_first = max(first - 128, 0)
        y_last = last if last == ny else last - 128
        y_width = y_last - y_first
        y_cols = pl.ds(y_first, y_width)
        more = pl.ds(y_first, min(y_width + 128, ny - y_first))
        for side in range(sides):
            piece_copy(side, p).wait_recv()
        u_next = ahead_of(u_ext[late + 1, :, more], y_width)
        v_next = [ahead_of(v_ext[side, late + 1, :, more], y_width) for side in range(sides)]
        columns = [stack(late + 1, cols) + stack(late, cols), stack(late + 2, cols) + stack(late + 1, cols),
                   [u_next, u_next, v_next[0], v_next[-1]] + stack(late + 1, y_cols)]
        diff = jnp.dot(pair, jnp.concatenate([jnp.concatenate(c, axis=0) for c in columns], axis=1),
                       preferred_element_type=jnp.float32)
        mid = weighted(diff[:, :width], kx_row(late - 1, cols))
        top = weighted(diff[:, width:2 * width], kx_row(late, cols))
        fy = weighted(diff[:, 2 * width:], lambda k: ky_ref[k, pl.ds(late, 1), y_cols])
        put(late - 1, cols, fx_prev[:, cols] - mid + held[:, cols])
        put(final, cols, last_row[:, cols] + top)
        if p == 0:
            lane = lax.broadcasted_iota(jnp.int32, fy.shape, 1)
            part = jnp.where(lane == 0, 0.0, pltpu.roll(fy, 1, axis=1)) - fy
            keep = mid - top
        else:
            both = jnp.concatenate([fy_row[:, y_first - 128:y_first], fy], axis=1)
            part = pltpu.roll(both, 1, axis=1)[:, 128:] - fy
            keep = jnp.concatenate([ahead[:, y_first:first], mid - top], axis=1)
        put(late, y_cols, keep[:, :y_width] + part)
        if last < ny:
            ahead[:, y_last:last] = keep[:, y_width:]
            fy_row[:, y_last - 128:y_last] = fy[:, y_width - 128:]

    for side in range(sides):
        pltpu.make_async_copy(raw, raw, field_send.at[side]).wait()
    coup_copy.wait_send()

    @pl.when(has_above)
    def _():
        strips(1 + sides, other_send.at[1]).wait()
        kx_copy.wait_send()

    @pl.when(has_below)
    def _():
        strips(1 + sides, other_send.at[2]).wait()


def shards(n_mode, n_space, field, kappa_x, kappa_y, coupling, pattern):
    mb, rows, ny = field.shape
    terms = kappa_x.shape[0]
    sides = 1 if n_mode == 2 else 2
    vmem = pl.BlockSpec(memory_space=pltpu.VMEM)
    hbm = pl.BlockSpec(memory_space=pltpu.HBM)
    out = pl.pallas_call(
        functools.partial(kernel, n_mode, n_space),
        out_shape=jax.ShapeDtypeStruct((mb * rows * ny // 128, 128), jnp.float32),
        in_specs=[hbm] * 5,
        out_specs=vmem,
        scratch_shapes=[
            pltpu.VMEM(field.shape, jnp.bfloat16),
            pltpu.VMEM((sides, mb, rows, min(EARLY, ny // 2)), jnp.bfloat16),
            pltpu.VMEM((mb * rows, 128), jnp.float32),
            pltpu.VMEM((rows + 2, mb, ny), jnp.bfloat16),
            pltpu.VMEM((sides, rows + 2, mb, ny), jnp.bfloat16),
            pltpu.VMEM((2,) + kappa_x.shape, jnp.float32),
            pltpu.VMEM(coupling.shape, jnp.bfloat16),
            pltpu.VMEM(pattern.shape, jnp.int32),
            pltpu.VMEM((terms * mb * mb // 128, 128), jnp.bfloat16),
            pltpu.VMEM((terms * mb * mb // 128, 128), jnp.bfloat16),
            pltpu.VMEM((terms * mb, 8 * mb), jnp.bfloat16),
            pltpu.VMEM((terms, 8, ny), jnp.float32),
            pltpu.VMEM((mb, ny), jnp.float32),
            pltpu.VMEM((mb, ny), jnp.float32),
            pltpu.VMEM((mb, ny), jnp.float32),
            pltpu.VMEM((mb, ny), jnp.float32),
            pltpu.VMEM((mb, ny), jnp.float32),
            pltpu.VMEM((mb, ny), jnp.float32),
            pltpu.VMEM((1 + sides, mb, ny), jnp.bfloat16),
            pltpu.SemaphoreType.DMA((4,)),
            pltpu.SemaphoreType.DMA((sides,)),
            pltpu.SemaphoreType.DMA((sides,)),
            pltpu.SemaphoreType.DMA((sides, rows // 2 + 1)),
            pltpu.SemaphoreType.DMA((sides, 1 + len(LATE))),
            pltpu.SemaphoreType.DMA((4,)),
            pltpu.SemaphoreType.DMA((5,)),
        ],
        compiler_params=pltpu.CompilerParams(collective_id=0, has_side_effects=True, vmem_limit_bytes=24 * 2**20),
    )(*[pltpu.with_memory_space_constraint(x, pltpu.HBM)
        for x in (field, kappa_x, kappa_y, coupling, pattern)])
    tiles = out.reshape(mb, rows // 8, ny // 128, 8, 128)
    return jnp.swapaxes(tiles, 2, 3).reshape(mb, rows, ny)


def solution(mesh):
    placed = (
        P("mode", "space", None),
        P(None, "space", None),
        P(None, "space", None),
        P("mode", None, None, None),
        P("mode", None, None, None),
    )
    return jax.shard_map(
        functools.partial(shards, mesh.shape["mode"], mesh.shape["space"]),
        mesh=mesh, in_specs=placed, out_specs=P("mode", "space", None), check_vma=False)
```

time: 31.6 us -> 29.9 us (0.946)
  Pallas kernels: 30.1 us -> 28.4 us
    pallas_call x1, Pallas kernels: 30.1 us -> 28.4 us  [shards(): pl.pallas_call(functools.partial(kernel, n_mode, n_space), out_shape=jax....]
where the time goes in v2:
time: 29.9 us; the launch traced here: 29.8 us
  Pallas kernels  28.4 us (95%)
  local copies, waits for them, and re-layouts  1.32 us (4%)
    pallas_call x1, Pallas kernels, shards(): pl.pallas_call(functools.partial(kernel, n_mode, n_space), out_shape=jax....  28.4 us
    unnamed x1, local copies, waits for them, and re-layouts  1.32 us

profile of v2, /device:TPU:0, one launch (start us, length us, event | category | flops | bytes accessed | tf_op | source)
XLA Modules:
  0.0 29.8 jit_solution(470243909690908102)
XLA Ops:
  0.0 28.4 %shard_map.55 = f32[4096,128]{1,0:T(8,128)S(1)} custom-call(bf16[32,16,1024]{2,1,0:T(8,128)(2,1)} %field_hbm.1, f32[8,16,1024]{2,1,0:T(8,128)} %kx_hbm.1, f32[8,16,1024]{2,1,0:T(8,128)} %ky_hbm.1, bf16[2,8,32,32]{3,2,1,0:T(8,128)(2,1)} %coup_hbm.1, s32[2,8,32,32]{3,2,1,0:T(8,128)} %pat_hbm.1), custom_call_target="tpu_custom_call" | custom-call | tf_op jit(solution)/shard_map/pallas_call | solution.py:347
  28.4 1.3 %copy.7 = f32[32,16,1024]{2,1,0:T(8,128)} copy(f32[32,16,1024]{2,1,0:T(8,128)S(1)} %bitcast.5) | data formatting | bytes 4194304

commit v3 on v2

v3 whole, which is shorter than its diff:
```python
import functools

import jax
import jax.numpy as jnp
from jax import lax
from jax.experimental import pallas as pl
from jax.experimental.pallas import tpu as pltpu
from jax.sharding import PartitionSpec as P

LANES = 256
PART = 16
EARLY = 128
LATE = (384,)


def kernel(n_mode, n_space, field_hbm, kx_hbm, ky_hbm, coup_hbm, pat_hbm, out_ref,
           raw, raw_in, tall, u_ext, v_ext, kappa, ky_left, coup, pat, packed, packed_in, relay, own_ref, mixed_ref, coef_ref,
           kx_in, pend, low, q_row, z_row, first_row, last_row, high,
           local_sem, field_send, early_recv, row_recv, piece_recv, other_send, other_recv, relay_sem, hello):
    mb, rows, ny = field_hbm.shape
    group = 128 // mb
    terms = kx_hbm.shape[0]
    sides = v_ext.shape[0]
    early = raw_in.shape[-1]
    mode = lax.axis_index("mode")
    space = lax.axis_index("space")
    above = {"space": lax.rem(space + 1, n_space)}
    below = {"space": lax.rem(space + n_space - 1, n_space)}
    upper = {"mode": lax.rem(mode + 1, n_mode)}
    lower = {"mode": lax.rem(mode + n_mode - 1, n_mode)}
    has_below = space > 0
    has_above = space < n_space - 1
    kx_ref, ky_ref = kappa.at[0], kappa.at[1]

    barrier = pltpu.get_barrier_semaphore()

    def greet(target):
        pl.semaphore_signal(barrier, inc=1, device_id=target, device_id_type=pl.DeviceIdType.MESH)

    for target in (upper, lower)[:sides]:
        greet(target)
    pl.when(has_above)(lambda: greet(above))

    field_load = pltpu.make_async_copy(field_hbm, raw, local_sem.at[0])
    coup_load = pltpu.make_async_copy(coup_hbm, coup, local_sem.at[1])
    pat_load = pltpu.make_async_copy(pat_hbm, pat, local_sem.at[2])
    kx_load = pltpu.make_async_copy(kx_hbm, kx_ref, local_sem.at[3])
    ky_load = pltpu.make_async_copy(ky_hbm, ky_ref, local_sem.at[3])
    for copy in (field_load, coup_load, pat_load, kx_load, ky_load):
        copy.start()

    def masked(slot, k):
        return jnp.where(pat[slot, k] > 0, coup[slot, k].astype(jnp.float32), 0.0)

    def placed(block, shape, offset, flip=False):
        spot = lax.broadcasted_iota(jnp.int32, shape, 0) + offset
        place = jnp.where(lax.broadcasted_iota(jnp.int32, shape, 1) == spot, 1.0, 0.0).astype(jnp.bfloat16)
        return lax.dot_general(block.astype(jnp.bfloat16), place, (((0 if flip else 1,), (0,)), ((), ())),
                               preferred_element_type=jnp.float32)

    def by_rows(source, target, first, count, width):
        for c in range(0, width, 128):
            tall[:mb * count] = source[:, first:first + count, c:c + 128].astype(jnp.float32).reshape(mb * count, 128)
            for r in range(count):
                target[first + r + 1, :, c:c + 128] = tall[pl.ds(r, mb, stride=count), :].astype(jnp.bfloat16)

    pl.semaphore_wait(barrier, sides + jnp.where(has_below, 1, 0))

    @pl.when(has_below)
    def _():
        pl.semaphore_signal(hello, inc=1, device_id=below, device_id_type=pl.DeviceIdType.MESH)

    def remote(src, dst, send, recv, target):
        return pltpu.make_async_remote_copy(
            src_ref=src, dst_ref=dst, send_sem=send, recv_sem=recv,
            device_id=target, device_id_type=pl.DeviceIdType.MESH)

    towards = (lower, upper)
    cuts = [early] + [ny - w for w in LATE if ny - w > early] + [ny]
    pieces = list(zip(cuts[:-1], cuts[1:]))
    pairs = (rows - 6) // 2
    rest = pl.ds(early, ny - early)

    def rows_copy(side, first, count, at, cols=rest, recv=row_recv):
        part = pl.ds(first + 1, count)
        return remote(u_ext.at[part, :, cols], v_ext.at[side, part, :, cols],
                      field_send.at[side], recv.at[side, at], towards[side])

    def pair_copy(side, h):
        return rows_copy(side, 2 * h + 2, 2, h + 2)

    def single_copy(side, r):
        return rows_copy(side, r, 1, r - (rows - 4) + pairs + 2)

    def piece_copy(side, p):
        first, last = pieces[p]
        return rows_copy(side, rows - 2, 1, p, pl.ds(first, last - first), piece_recv)

    def early_copy(side):
        return remote(field_hbm.at[:, :, pl.ds(0, early)], raw_in.at[side], field_send.at[side], early_recv.at[side], towards[side])

    def halo_up(side):
        return remote(v_ext.at[side, rows], v_ext.at[side, 0], other_send.at[1], other_recv.at[1], above)

    def halo_down(side):
        return remote(v_ext.at[side, 1], v_ext.at[side, rows + 1], other_send.at[2], other_recv.at[2], below)

    shared = n_space % 2 == 0
    sends_coup = lax.rem(space, 2) == 0 if shared else space >= 0
    coup_pass = remote(packed_in, packed_in, other_send.at[4], other_recv.at[0], above)
    coup_copy = remote(packed, packed_in, other_send.at[0], other_recv.at[0], upper)
    last_copy = remote(u_ext.at[rows], u_ext.at[0], other_send.at[1], other_recv.at[1], above)
    first_copy = remote(u_ext.at[1], u_ext.at[rows + 1], other_send.at[2], other_recv.at[2], below)
    kx_copy = remote(kx_hbm.at[:, pl.ds(rows - 8, 8), :], kx_in, other_send.at[3], other_recv.at[3], above)

    def strips(count, sem):
        part = u_ext.at[pl.ds(0, count)]
        return pltpu.make_async_copy(part, part, sem)

    for side in range(sides):
        early_copy(side).start()

    coup_load.wait()
    pat_load.wait()

    @pl.when(sends_coup)
    def _():
        for q in range(terms // group):
            beside = None
            for p in range(group):
                part = placed(masked(1, q * group + p), (mb, 128), p * mb, flip=True)
                beside = part if beside is None else beside + part
            packed[q * mb:(q + 1) * mb] = beside.astype(jnp.bfloat16)
        coup_copy.start()

    field_load.wait()
    by_rows(raw, u_ext, 0, rows, ny)
    pl.when(has_above)(lambda: pl.semaphore_wait(hello, 1))

    detour = sides == 1 and n_space > 2
    gone = rows - 3
    source = (mode == 1) & (space == 1)
    middle = (mode == 1) & (space == 2)
    turn = (mode == 0) & (space == 2)
    yields = (mode == 1) & ((space == 1) | (space == 3))
    leave_copy = remote(u_ext.at[pl.ds(gone + 1, 1), :, rest], relay, field_send.at[0], relay_sem.at[0], above)
    cross_copy = remote(relay, relay, relay_sem.at[1], relay_sem.at[0], upper)
    come_copy = remote(relay, v_ext.at[0, pl.ds(gone + 1, 1), :, rest], relay_sem.at[1], row_recv.at[0, pairs + 3], below)

    if detour:
        pl.when(source)(leave_copy.start)
    for side in range(sides):
        rows_copy(side, 0, 2, 0).start()
    pl.when(has_below)(first_copy.start)
    if detour:
        @pl.when(middle)
        def _():
            leave_copy.wait_recv()
            cross_copy.start()
    for side in range(sides):
        rows_copy(side, rows - 1, 1, 1).start()
    if detour:
        @pl.when(turn)
        def _():
            cross_copy.wait_recv()
            come_copy.start()

    def send_rest():
        for side in range(sides):
            @pl.loop(0, pairs)
            def _(h):
                pair_copy(side, h).start()
        for r in (rows - 4, rows - 3):
            for side in range(sides):
                if detour and r == gone:
                    pl.when(jnp.logical_not(source))(single_copy(side, r).start)
                else:
                    single_copy(side, r).start()
        for p in range(len(pieces)):
            for side in range(sides):
                piece_copy(side, p).start()

        @pl.when(has_above)
        def _():
            last_copy.start()
            kx_copy.start()

    if detour:
        pl.when(jnp.logical_not(yields))(send_rest)
    else:
        send_rest()

    for k in range(terms):
        half = masked(0, k) * 0.5
        shape = (mb, 4 * mb)
        coef = placed(half, shape, 0) + placed(half, shape, mb, flip=True) + placed(masked(1, k), shape, 2 * mb)
        own_ref[k * mb:(k + 1) * mb] = coef

    for side in range(sides):
        early_copy(side).wait_recv()
    for side in range(sides):
        by_rows(raw_in.at[side], v_ext.at[side], 0, rows, early)
    coup_copy.wait_recv()
    if shared:
        pl.when(sends_coup)(coup_pass.start)
    pltpu.make_async_copy(kappa, kappa, local_sem.at[3]).wait()
    for k in range(terms):
        lane = lax.broadcasted_iota(jnp.int32, (rows, ny), 1)
        ky_left[k] = jnp.where(lane == 0, 0.0, pltpu.roll(ky_ref[k], 1, axis=1))
    for k in range(terms):
        q, p = divmod(k, group)
        shape = (mb, 4 * mb)
        coef = (own_ref[k * mb:(k + 1) * mb]
                + placed(packed_in[q * mb:(q + 1) * mb, p * mb:(p + 1) * mb], shape, 3 * mb))
        for m in range(0, mb, PART):
            own_at = m * terms + k * PART
            mixed_ref[own_at:own_at + PART] = coef[m:m + PART]
    coef_ref[...] = mixed_ref[...].astype(jnp.bfloat16)
    for side in range(sides):
        rows_copy(side, 0, 2, 0).wait_recv()
        pl.when(has_below)(halo_down(side).start)
    if detour:
        pl.when(yields)(send_rest)
    for side in range(sides):
        rows_copy(side, rows - 1, 1, 1).wait_recv()
        pl.when(has_above)(halo_up(side).start)

    coef = coef_ref[...]
    final = rows - 1
    late = rows - 2

    def w_of(e, cols):
        u = u_ext[e, :, cols]
        vs = [v_ext[side, e, :, cols] for side in range(sides)]
        return jnp.dot(coef, jnp.concatenate([u, u, vs[0], vs[-1]], axis=0), preferred_element_type=jnp.float32)

    def sums(w, *weights):
        parts = [[] for _ in weights]
        scales = [[weight(k) for k in range(terms)] for weight in weights]
        for m in range(0, mb, PART):
            totals = [None] * len(weights)
            for k in range(terms):
                part = w[m * terms + k * PART:m * terms + (k + 1) * PART]
                for i in range(len(weights)):
                    value = scales[i][k] * part
                    totals[i] = value if totals[i] is None else totals[i] + value
            for i in range(len(weights)):
                parts[i].append(totals[i])
        return [jnp.concatenate(p, axis=0) for p in parts]

    def row_of(ref, r, cols):
        return lambda k: ref[k, pl.ds(r, 1), cols]

    def from_left(q):
        lane = lax.broadcasted_iota(jnp.int32, q.shape, 1)
        return jnp.where(lane == 0, 0.0, pltpu.roll(q, 1, axis=1))

    def from_right(z):
        lane = lax.broadcasted_iota(jnp.int32, z.shape, 1)
        return jnp.where(lane == z.shape[1] - 1, 0.0, pltpu.roll(z, z.shape[1] - 1, axis=1))

    blocks = [pl.ds(c, LANES) for c in range(0, ny, LANES)]

    def put(r, cols, value):
        for at in range(0, cols.size, 128):
            tile = (cols.start + at) // 128
            start = (r // 8) * 8 * (ny // 128) + tile * 8 + r % 8
            out_ref[pl.ds(start, mb, stride=rows * (ny // 128)), :] = value[:, at:at + 128]

    def row_step(r, give):
        for cols in blocks:
            a, b, q, z = sums(w_of(r + 1, cols), row_of(kx_ref, r - 1, cols), row_of(kx_ref, r, cols),
                              row_of(ky_ref, r, cols), row_of(ky_left, r, cols))
            give(cols, a)
            pend[:, cols] = a + b + q + z - low[:, cols]
            low[:, cols] = b
            q_row[:, cols] = q
            z_row[:, cols] = z
        pend[...] = pend[...] - from_left(q_row[...]) - from_right(z_row[...])

    def full_step(r):
        row_step(r, lambda cols, a: put(r - 1, cols, pend[:, cols] - a))

    def edges():
        @pl.when(has_below)
        def _():
            strips(1 + sides, other_recv.at[1]).wait()
            kx_copy.wait_recv()

        @pl.when(has_above)
        def _():
            strips(1 + sides, other_recv.at[2]).wait()

        def blank(e):
            u_ext[e] = jnp.zeros((mb, ny), jnp.bfloat16)
            for side in range(sides):
                v_ext[side, e] = jnp.zeros((mb, ny), jnp.bfloat16)

        @pl.when(jnp.logical_not(has_below))
        def _():
            blank(0)
            kx_in[...] = jnp.zeros_like(kx_in)

        @pl.when(jnp.logical_not(has_above))
        def _():
            blank(rows + 1)

        for cols in blocks:
            outer = lambda k: kx_in[k, 7:8, cols]
            put(0, cols, first_row[:, cols] + sums(w_of(1, cols), outer)[0] - sums(w_of(0, cols), outer)[0])
            a, b, q, z = sums(w_of(rows, cols), row_of(kx_ref, late, cols), row_of(kx_ref, final, cols),
                              row_of(ky_ref, final, cols), row_of(ky_left, final, cols))
            last_row[:, cols] = a + b + q + z - sums(w_of(rows + 1, cols), row_of(kx_ref, final, cols))[0]
            high[:, cols] = a
            first_row[:, cols] = q
            z_row[:, cols] = z
        last_row[...] = last_row[...] - from_left(first_row[...]) - from_right(z_row[...])

    for cols in blocks:
        b, q, z = sums(w_of(1, cols), row_of(kx_ref, 0, cols), row_of(ky_ref, 0, cols), row_of(ky_left, 0, cols))
        low[:, cols] = b
        first_row[:, cols] = b + q + z
        q_row[:, cols] = q
        z_row[:, cols] = z
    first_row[...] = first_row[...] - from_left(q_row[...]) - from_right(z_row[...])

    def take_first(cols, a):
        first_row[:, cols] = first_row[:, cols] - a

    row_step(1, take_first)

    @pl.loop(0, pairs)
    def _(h):
        pl.when(h == pairs // 2)(edges)
        for side in range(sides):
            pair_copy(side, h).wait_recv()
        full_step(2 * h + 2)
        full_step(2 * h + 3)

    @pl.loop(rows - 4, rows - 2)
    def _(r):
        for side in range(sides):
            single_copy(side, r).wait_recv()
        full_step(r)

    high[...] = high[...] + low[...]

    for p, (first, last) in enumerate(pieces):
        first = 0 if p == 0 else first
        width = last - first
        cols = pl.ds(first, width)
        for side in range(sides):
            piece_copy(side, p).wait_recv()
        a, b, q, z = sums(w_of(late + 1, cols), row_of(kx_ref, late - 1, cols), row_of(kx_ref, late, cols),
                          row_of(ky_ref, late, cols), row_of(ky_left, late, cols))
        put(late - 1, cols, pend[:, cols] - a)
        put(final, cols, last_row[:, cols] - b)
        total = a + b + q + z - high[:, cols]
        y_first = max(first - 128, 0)
        y_last = last if last == ny else last - 128
        y_width = y_last - y_first
        if p > 0:
            before = pl.ds(y_first, 128)
            total = jnp.concatenate([low[:, before], total], axis=1)
            z = jnp.concatenate([z_row[:, before], z], axis=1)
            left = pltpu.roll(jnp.concatenate([q_row[:, y_first - 128:first], q], axis=1), 1, axis=1)[:, 128:]
        else:
            left = from_left(q)
        right = from_right(z) if last == ny else pltpu.roll(z, z.shape[1] - 1, axis=1)
        put(late, pl.ds(y_first, y_width), (total - left - right)[:, :y_width])
        if last < ny:
            after = pl.ds(y_last, 128)
            low[:, after] = total[:, y_width:]
            z_row[:, after] = z[:, y_width:]
            q_row[:, y_last - 128:last] = q[:, q.shape[1] - 256:]

    for side in range(sides):
        pltpu.make_async_copy(raw, raw, field_send.at[side]).wait()
    if detour:
        pl.when(middle | turn)(cross_copy.wait_send)

    @pl.when(sends_coup)
    def _():
        coup_copy.wait_send()
        if shared:
            coup_pass.wait_send()

    @pl.when(has_above)
    def _():
        strips(1 + sides, other_send.at[1]).wait()
        kx_copy.wait_send()

    @pl.when(has_below)
    def _():
        strips(1 + sides, other_send.at[2]).wait()


def shards(n_mode, n_space, field, kappa_x, kappa_y, coupling, pattern):
    mb, rows, ny = field.shape
    terms = kappa_x.shape[0]
    sides = 1 if n_mode == 2 else 2
    vmem = pl.BlockSpec(memory_space=pltpu.VMEM)
    hbm = pl.BlockSpec(memory_space=pltpu.HBM)
    out = pl.pallas_call(
        functools.partial(kernel, n_mode, n_space),
        out_shape=jax.ShapeDtypeStruct((mb * rows * ny // 128, 128), jnp.float32),
        in_specs=[hbm] * 5,
        out_specs=vmem,
        scratch_shapes=[
            pltpu.VMEM(field.shape, jnp.bfloat16),
            pltpu.VMEM((sides, mb, rows, min(EARLY, ny // 2)), jnp.bfloat16),
            pltpu.VMEM((mb * rows, 128), jnp.float32),
            pltpu.VMEM((rows + 2, mb, ny), jnp.bfloat16),
            pltpu.VMEM((sides, rows + 2, mb, ny), jnp.bfloat16),
            pltpu.VMEM((2,) + kappa_x.shape, jnp.float32),
            pltpu.VMEM(kappa_y.shape, jnp.float32),
            pltpu.VMEM(coupling.shape, jnp.bfloat16),
            pltpu.VMEM(pattern.shape, jnp.int32),
            pltpu.VMEM((terms * mb * mb // 128, 128), jnp.bfloat16),
            pltpu.VMEM((terms * mb * mb // 128, 128), jnp.bfloat16),
            pltpu.VMEM((1, mb, ny - min(EARLY, ny // 2)), jnp.bfloat16),
            pltpu.VMEM((terms * mb, 4 * mb), jnp.float32),
            pltpu.VMEM((terms * mb, 4 * mb), jnp.float32),
            pltpu.VMEM((terms * mb, 4 * mb), jnp.bfloat16),
            pltpu.VMEM((terms, 8, ny), jnp.float32),
            pltpu.VMEM((mb, ny), jnp.float32),
            pltpu.VMEM((mb, ny), jnp.float32),
            pltpu.VMEM((mb, ny), jnp.float32),
            pltpu.VMEM((mb, ny), jnp.float32),
            pltpu.VMEM((mb, ny), jnp.float32),
            pltpu.VMEM((mb, ny), jnp.float32),
            pltpu.VMEM((mb, ny), jnp.float32),
            pltpu.SemaphoreType.DMA((4,)),
            pltpu.SemaphoreType.DMA((sides,)),
            pltpu.SemaphoreType.DMA((sides,)),
            pltpu.SemaphoreType.DMA((sides, rows // 2 + 1)),
            pltpu.SemaphoreType.DMA((sides, 1 + len(LATE))),
            pltpu.SemaphoreType.DMA((5,)),
            pltpu.SemaphoreType.DMA((4,)),
            pltpu.SemaphoreType.DMA((2,)),
            pltpu.SemaphoreType.REGULAR,
        ],
        compiler_params=pltpu.CompilerParams(collective_id=0, has_side_effects=True, vmem_limit_bytes=24 * 2**20),
    )(*[pltpu.with_memory_space_constraint(x, pltpu.HBM)
        for x in (field, kappa_x, kappa_y, coupling, pattern)])
    tiles = out.reshape(mb, rows // 8, ny // 128, 8, 128)
    return jnp.swapaxes(tiles, 2, 3).reshape(mb, rows, ny)


def solution(mesh):
    placed = (
        P("mode", "space", None),
        P(None, "space", None),
        P(None, "space", None),
        P("mode", None, None, None),
        P("mode", None, None, None),
    )
    return jax.shard_map(
        functools.partial(shards, mesh.shape["mode"], mesh.shape["space"]),
        mesh=mesh, in_specs=placed, out_specs=P("mode", "space", None), check_vma=False)
```

time: 29.9 us -> 28.9 us (0.967); the launches traced: 29.8 us -> 28.4 us
  Pallas kernels: 28.4 us -> 27.1 us
    pallas_call x1, Pallas kernels: 28.4 us -> 27.1 us  [shards(): pl.pallas_call(functools.partial(kernel, n_mode, n_space), out_shape=jax....]
where the time goes in v3:
time: 28.9 us; the launch traced here: 28.4 us
  Pallas kernels  27.1 us (94%)
  local copies, waits for them, and re-layouts  1.32 us (5%)
    pallas_call x1, Pallas kernels, shards(): pl.pallas_call(functools.partial(kernel, n_mode, n_space), out_shape=jax....  27.1 us
    unnamed x1, local copies, waits for them, and re-layouts  1.32 us

profile of v3, /device:TPU:0, one launch (start us, length us, event | category | flops | bytes accessed | tf_op | source)
XLA Modules:
  0.0 28.4 jit_solution(8060185441679562925)
XLA Ops:
  0.0 27.1 %shard_map.55 = f32[4096,128]{1,0:T(8,128)S(1)} custom-call(bf16[32,16,1024]{2,1,0:T(8,128)(2,1)} %field_hbm.1, f32[8,16,1024]{2,1,0:T(8,128)} %kx_hbm.1, f32[8,16,1024]{2,1,0:T(8,128)} %ky_hbm.1, bf16[2,8,32,32]{3,2,1,0:T(8,128)(2,1)} %coup_hbm.1, s32[2,8,32,32]{3,2,1,0:T(8,128)} %pat_hbm.1), custom_call_target="tpu_custom_call" | custom-call | tf_op jit(solution)/shard_map/pallas_call | solution.py:404
  27.1 1.3 %copy.7 = f32[32,16,1024]{2,1,0:T(8,128)} copy(f32[32,16,1024]{2,1,0:T(8,128)S(1)} %bitcast.5) | data formatting | bytes 4194304

commit v4 on v3

--- a/solution.py
+++ b/solution.py
@@ -11,6 +11,7 @@
 PART = 16
 EARLY = 128
 LATE = (384,)
+ASIDE = 384
 
 
 def kernel(n_mode, n_space, field_hbm, kx_hbm, ky_hbm, coup_hbm, pat_hbm, out_ref,
@@ -87,10 +88,13 @@
                       field_send.at[side], recv.at[side, at], towards[side])
 
     def pair_copy(side, h):
-        return rows_copy(side, 2 * h + 2, 2, h + 2)
-
-    def single_copy(side, r):
-        return rows_copy(side, r, 1, r - (rows - 4) + pairs + 2)
+        return rows_copy(side, 2 * h + 3, 2, h + 4)
+
+    def early_row(side):
+        return rows_copy(side, 2, 1, 2)
+
+    def late_row(side):
+        return rows_copy(side, rows - 3, 1, 3)
 
     def piece_copy(side, p):
         first, last = pieces[p]
@@ -137,45 +141,57 @@
     by_rows(raw, u_ext, 0, rows, ny)
     pl.when(has_above)(lambda: pl.semaphore_wait(hello, 1))
 
-    detour = sides == 1 and n_space > 2
-    gone = rows - 3
-    source = (mode == 1) & (space == 1)
-    middle = (mode == 1) & (space == 2)
-    turn = (mode == 0) & (space == 2)
-    yields = (mode == 1) & ((space == 1) | (space == 3))
-    leave_copy = remote(u_ext.at[pl.ds(gone + 1, 1), :, rest], relay, field_send.at[0], relay_sem.at[0], above)
-    cross_copy = remote(relay, relay, relay_sem.at[1], relay_sem.at[0], upper)
-    come_copy = remote(relay, v_ext.at[0, pl.ds(gone + 1, 1), :, rest], relay_sem.at[1], row_recv.at[0, pairs + 3], below)
-
-    if detour:
+    detours = [(1, ny - early), (3, min(ASIDE, ny - early))] if sides == 1 and n_space > 4 else []
+    strong = (mode == 1) & ((space == 1) | (space == 3))
+    weak = (mode == 1) & (lax.rem(space, 2) == 1) & (space > 3)
+    yields = strong | weak if detours else space < 0
+    hops = []
+    for at, width in detours:
+        part = pl.ds(early, width)
+        held_part = relay.at[:, :, pl.ds(0, width)]
+        hops.append((
+            (mode == 1) & (space == at), (mode == 1) & (space == at + 1), (mode == 0) & (space == at + 1),
+            remote(u_ext.at[pl.ds(3, 1), :, part], held_part, field_send.at[0], relay_sem.at[0], above),
+            remote(held_part, held_part, relay_sem.at[1], relay_sem.at[0], upper),
+            remote(held_part, v_ext.at[0, pl.ds(3, 1), :, part], relay_sem.at[1], row_recv.at[0, 2], below)))
+
+    def early_rows(here):
+        whole = here
+        for (at, width), hop in zip(detours, hops):
+            whole = whole & jnp.logical_not(hop[0])
+            if width < ny - early:
+                pl.when(here & hop[0])(rows_copy(0, 2, 1, 2, pl.ds(early + width, ny - early - width)).start)
+        for side in range(sides):
+            pl.when(whole)(early_row(side).start)
+
+    for source, _, _, leave_copy, _, _ in hops:
         pl.when(source)(leave_copy.start)
     for side in range(sides):
         rows_copy(side, 0, 2, 0).start()
     pl.when(has_below)(first_copy.start)
-    if detour:
+    for _, middle, _, leave_copy, cross_copy, _ in hops:
         @pl.when(middle)
         def _():
             leave_copy.wait_recv()
             cross_copy.start()
     for side in range(sides):
         rows_copy(side, rows - 1, 1, 1).start()
-    if detour:
+    early_rows(jnp.logical_not(strong))
+    for _, _, turn, _, cross_copy, come_copy in hops:
         @pl.when(turn)
         def _():
             cross_copy.wait_recv()
             come_copy.start()
 
     def send_rest():
+        if detours:
+            early_rows(strong)
         for side in range(sides):
             @pl.loop(0, pairs)
             def _(h):
                 pair_copy(side, h).start()
-        for r in (rows - 4, rows - 3):
-            for side in range(sides):
-                if detour and r == gone:
-                    pl.when(jnp.logical_not(source))(single_copy(side, r).start)
-                else:
-                    single_copy(side, r).start()
+        for side in range(sides):
+            late_row(side).start()
         for p in range(len(pieces)):
             for side in range(sides):
                 piece_copy(side, p).start()
@@ -185,10 +201,7 @@
             last_copy.start()
             kx_copy.start()
 
-    if detour:
-        pl.when(jnp.logical_not(yields))(send_rest)
-    else:
-        send_rest()
+    pl.when(jnp.logical_not(yields))(send_rest)
 
     for k in range(terms):
         half = masked(0, k) * 0.5
@@ -219,7 +232,7 @@
     for side in range(sides):
         rows_copy(side, 0, 2, 0).wait_recv()
         pl.when(has_below)(halo_down(side).start)
-    if detour:
+    if detours:
         pl.when(yields)(send_rest)
     for side in range(sides):
         rows_copy(side, rows - 1, 1, 1).wait_recv()
@@ -329,19 +342,21 @@
 
     row_step(1, take_first)
 
+    for side in range(sides):
+        early_row(side).wait_recv()
+    full_step(2)
+
     @pl.loop(0, pairs)
     def _(h):
         pl.when(h == pairs // 2)(edges)
         for side in range(sides):
             pair_copy(side, h).wait_recv()
-        full_step(2 * h + 2)
         full_step(2 * h + 3)
-
-    @pl.loop(rows - 4, rows - 2)
-    def _(r):
-        for side in range(sides):
-            single_copy(side, r).wait_recv()
-        full_step(r)
+        full_step(2 * h + 4)
+
+    for side in range(sides):
+        late_row(side).wait_recv()
+    full_step(rows - 3)
 
     high[...] = high[...] + low[...]
 
@@ -376,7 +391,7 @@
 
     for side in range(sides):
         pltpu.make_async_copy(raw, raw, field_send.at[side]).wait()
-    if detour:
+    for _, middle, turn, _, cross_copy, _ in hops:
         pl.when(middle | turn)(cross_copy.wait_send)
 
     @pl.when(sends_coup)

time: 28.9 us -> 28.6 us (0.990)
  no operation moved by 1% of the time
where the time goes in v4:
time: 28.6 us; the launch traced here: 28.4 us
  Pallas kernels  27 us (94%)
  local copies, waits for them, and re-layouts  1.32 us (5%)
    pallas_call x1, Pallas kernels, shards(): pl.pallas_call(functools.partial(kernel, n_mode, n_space), out_shape=jax....  27 us
    unnamed x1, local copies, waits for them, and re-layouts  1.32 us

profile of v4, /device:TPU:0, one launch (start us, length us, event | category | flops | bytes accessed | tf_op | source)
XLA Modules:
  0.0 28.4 jit_solution(1171702684094028884)
XLA Ops:
  0.0 27.0 %shard_map.55 = f32[4096,128]{1,0:T(8,128)S(1)} custom-call(bf16[32,16,1024]{2,1,0:T(8,128)(2,1)} %field_hbm.1, f32[8,16,1024]{2,1,0:T(8,128)} %kx_hbm.1, f32[8,16,1024]{2,1,0:T(8,128)} %ky_hbm.1, bf16[2,8,32,32]{3,2,1,0:T(8,128)(2,1)} %coup_hbm.1, s32[2,8,32,32]{3,2,1,0:T(8,128)} %pat_hbm.1), custom_call_target="tpu_custom_call" | custom-call | tf_op jit(solution)/shard_map/pallas_call | solution.py:419
  27.1 1.3 %copy.7 = f32[32,16,1024]{2,1,0:T(8,128)} copy(f32[32,16,1024]{2,1,0:T(8,128)S(1)} %bitcast.5) | data formatting | bytes 4194304

commit v5 on v4

--- a/solution.py
+++ b/solution.py
@@ -10,12 +10,67 @@
 LANES = 256
 PART = 16
 EARLY = 128
-LATE = (384,)
+LATE = 384
 ASIDE = 384
 
 
-def kernel(n_mode, n_space, field_hbm, kx_hbm, ky_hbm, coup_hbm, pat_hbm, out_ref,
-           raw, raw_in, tall, u_ext, v_ext, kappa, ky_left, coup, pat, packed, packed_in, relay, own_ref, mixed_ref, coef_ref,
+def weighted_sums(w, mb, terms, *weights):
+    parts = [[] for _ in weights]
+    scales = [[weight(k) for k in range(terms)] for weight in weights]
+    for m in range(0, mb, PART):
+        totals = [None] * len(weights)
+        for k in range(terms):
+            part = w[m * terms + k * PART:m * terms + (k + 1) * PART]
+            for i in range(len(weights)):
+                value = scales[i][k] * part
+                totals[i] = value if totals[i] is None else totals[i] + value
+        for i in range(len(weights)):
+            parts[i].append(totals[i])
+    return [jnp.concatenate(p, axis=0) for p in parts]
+
+
+def from_left(q):
+    lane = lax.broadcasted_iota(jnp.int32, q.shape, 1)
+    return jnp.where(lane == 0, 0.0, pltpu.roll(q, 1, axis=1))
+
+
+def from_right(z):
+    lane = lax.broadcasted_iota(jnp.int32, z.shape, 1)
+    return jnp.where(lane == z.shape[1] - 1, 0.0, pltpu.roll(z, z.shape[1] - 1, axis=1))
+
+
+def closing(rows, x_ref, coef_ref, ends_ref, rim_ref, scale_ref, out_ref, tail, sem):
+    mb = ends_ref.shape[1]
+    sides = ends_ref.shape[0] - 1
+    terms, width = scale_ref.shape[1:]
+    done = pl.ds(0, x_ref.shape[1] - tail.shape[1])
+    left_over = pl.ds(x_ref.shape[1] - tail.shape[1], tail.shape[1])
+    bulk = pltpu.make_async_copy(x_ref.at[:, done], out_ref.at[:, done], sem.at[0])
+    bulk.start()
+    tail[...] = x_ref[:, left_over]
+    flat = tail.reshape(mb * tail.shape[1], 128)
+
+    def put(r, first, value):
+        for at in range(0, value.shape[1], 128):
+            flat[pl.ds((first + at) // 16 + r % 8, mb, stride=tail.shape[1]), :] = value[:, at:at + 128]
+
+    u, vs = ends_ref[0], [ends_ref[1 + side] for side in range(sides)]
+    w = jnp.dot(coef_ref[...], jnp.concatenate([u, u, vs[0], vs[-1]], axis=0), preferred_element_type=jnp.float32)
+    a, b, q, z = weighted_sums(w, mb, terms, *[lambda k, i=i: scale_ref[i, k:k + 1, :] for i in range(4)])
+    put(rows - 3, 128, rim_ref[0, :, :width] - a)
+    put(rows - 1, 128, rim_ref[1, :, :width] - b)
+    total = jnp.concatenate([rim_ref[3, :, :128], a + b + q + z - rim_ref[2, :, :width]], axis=1)
+    left = pltpu.roll(jnp.concatenate([rim_ref[3, :, 256:512], q], axis=1), 1, axis=1)[:, 128:]
+    right = from_right(jnp.concatenate([rim_ref[3, :, 128:256], z], axis=1))
+    put(rows - 2, 0, total - left - right)
+    rest = pltpu.make_async_copy(tail, out_ref.at[:, left_over], sem.at[1])
+    rest.start()
+    bulk.wait()
+    rest.wait()
+
+
+def kernel(n_mode, n_space, field_hbm, kx_hbm, ky_hbm, coup_hbm, pat_hbm, out_ref, coef_ref, ends_ref, rim_ref, scale_ref,
+           raw, raw_in, tall, u_ext, v_ext, kappa, ky_left, coup, pat, packed, packed_in, relay, own_ref, mixed_ref,
            kx_in, pend, low, q_row, z_row, first_row, last_row, high,
            local_sem, field_send, early_recv, row_recv, piece_recv, other_send, other_recv, relay_sem, hello):
     mb, rows, ny = field_hbm.shape
@@ -77,8 +132,8 @@
             device_id=target, device_id_type=pl.DeviceIdType.MESH)
 
     towards = (lower, upper)
-    cuts = [early] + [ny - w for w in LATE if ny - w > early] + [ny]
-    pieces = list(zip(cuts[:-1], cuts[1:]))
+    split = ny - ends_ref.shape[-1]
+    pieces = [(early, split), (split, ny)]
     pairs = (rows - 6) // 2
     rest = pl.ds(early, ny - early)
 
@@ -248,29 +303,10 @@
         return jnp.dot(coef, jnp.concatenate([u, u, vs[0], vs[-1]], axis=0), preferred_element_type=jnp.float32)
 
     def sums(w, *weights):
-        parts = [[] for _ in weights]
-        scales = [[weight(k) for k in range(terms)] for weight in weights]
-        for m in range(0, mb, PART):
-            totals = [None] * len(weights)
-            for k in range(terms):
-                part = w[m * terms + k * PART:m * terms + (k + 1) * PART]
-                for i in range(len(weights)):
-                    value = scales[i][k] * part
-                    totals[i] = value if totals[i] is None else totals[i] + value
-            for i in range(len(weights)):
-                parts[i].append(totals[i])
-        return [jnp.concatenate(p, axis=0) for p in parts]
+        return weighted_sums(w, mb, terms, *weights)
 
     def row_of(ref, r, cols):
         return lambda k: ref[k, pl.ds(r, 1), cols]
-
-    def from_left(q):
-        lane = lax.broadcasted_iota(jnp.int32, q.shape, 1)
-        return jnp.where(lane == 0, 0.0, pltpu.roll(q, 1, axis=1))
-
-    def from_right(z):
-        lane = lax.broadcasted_iota(jnp.int32, z.shape, 1)
-        return jnp.where(lane == z.shape[1] - 1, 0.0, pltpu.roll(z, z.shape[1] - 1, axis=1))
 
     blocks = [pl.ds(c, LANES) for c in range(0, ny, LANES)]
 
@@ -360,34 +396,30 @@
 
     high[...] = high[...] + low[...]
 
-    for p, (first, last) in enumerate(pieces):
-        first = 0 if p == 0 else first
-        width = last - first
-        cols = pl.ds(first, width)
-        for side in range(sides):
-            piece_copy(side, p).wait_recv()
-        a, b, q, z = sums(w_of(late + 1, cols), row_of(kx_ref, late - 1, cols), row_of(kx_ref, late, cols),
-                          row_of(ky_ref, late, cols), row_of(ky_left, late, cols))
-        put(late - 1, cols, pend[:, cols] - a)
-        put(final, cols, last_row[:, cols] - b)
-        total = a + b + q + z - high[:, cols]
-        y_first = max(first - 128, 0)
-        y_last = last if last == ny else last - 128
-        y_width = y_last - y_first
-        if p > 0:
-            before = pl.ds(y_first, 128)
-            total = jnp.concatenate([low[:, before], total], axis=1)
-            z = jnp.concatenate([z_row[:, before], z], axis=1)
-            left = pltpu.roll(jnp.concatenate([q_row[:, y_first - 128:first], q], axis=1), 1, axis=1)[:, 128:]
-        else:
-            left = from_left(q)
-        right = from_right(z) if last == ny else pltpu.roll(z, z.shape[1] - 1, axis=1)
-        put(late, pl.ds(y_first, y_width), (total - left - right)[:, :y_width])
-        if last < ny:
-            after = pl.ds(y_last, 128)
-            low[:, after] = total[:, y_width:]
-            z_row[:, after] = z[:, y_width:]
-            q_row[:, y_last - 128:last] = q[:, q.shape[1] - 256:]
+    last = pieces[0][1]
+    cols = pl.ds(0, last)
+    for side in range(sides):
+        piece_copy(side, 0).wait_recv()
+    a, b, q, z = sums(w_of(late + 1, cols), row_of(kx_ref, late - 1, cols), row_of(kx_ref, late, cols),
+                      row_of(ky_ref, late, cols), row_of(ky_left, late, cols))
+    put(late - 1, cols, pend[:, cols] - a)
+    put(final, cols, last_row[:, cols] - b)
+    total = a + b + q + z - high[:, cols]
+    right = pltpu.roll(z, last - 1, axis=1)
+    put(late, pl.ds(0, last - 128), (total - from_left(q) - right)[:, :last - 128])
+    rim_ref[3, :, :128] = total[:, last - 128:]
+    rim_ref[3, :, 128:256] = z[:, last - 128:]
+    rim_ref[3, :, 256:512] = q[:, last - 256:]
+    end = pl.ds(last, ny - last)
+    for i, part in enumerate((pend, last_row, high)):
+        rim_ref[i, :, :ny - last] = part[:, end]
+    for k in range(terms):
+        for i, (part, r) in enumerate(((kx_ref, late - 1), (kx_ref, late), (ky_ref, late), (ky_left, late))):
+            scale_ref[i, k:k + 1, :] = part[k, r:r + 1, end]
+    ends_ref[0] = u_ext[late + 1, :, end]
+    for side in range(sides):
+        piece_copy(side, 1).wait_recv()
+        ends_ref[1 + side] = v_ext[side, late + 1, :, end]
 
     for side in range(sides):
         pltpu.make_async_copy(raw, raw, field_send.at[side]).wait()
@@ -416,11 +448,19 @@
     sides = 1 if n_mode == 2 else 2
     vmem = pl.BlockSpec(memory_space=pltpu.VMEM)
     hbm = pl.BlockSpec(memory_space=pltpu.HBM)
-    out = pl.pallas_call(
+    across = rows * ny // 128
+    width = min(LATE, ny - 512)
+    results = pl.pallas_call(
         functools.partial(kernel, n_mode, n_space),
-        out_shape=jax.ShapeDtypeStruct((mb * rows * ny // 128, 128), jnp.float32),
+        out_shape=[
+            jax.ShapeDtypeStruct((mb * across, 128), jnp.float32),
+            jax.ShapeDtypeStruct((terms * mb, 4 * mb), jnp.bfloat16),
+            jax.ShapeDtypeStruct((1 + sides, mb, width), jnp.bfloat16),
+            jax.ShapeDtypeStruct((4, mb, 512), jnp.float32),
+            jax.ShapeDtypeStruct((4, terms, width), jnp.float32),
+        ],
         in_specs=[hbm] * 5,
-        out_specs=vmem,
+        out_specs=[vmem] * 5,
         scratch_shapes=[
             pltpu.VMEM(field.shape, jnp.bfloat16),
             pltpu.VMEM((sides, mb, rows, min(EARLY, ny // 2)), jnp.bfloat16),
@@ -436,7 +476,6 @@
             pltpu.VMEM((1, mb, ny - min(EARLY, ny // 2)), jnp.bfloat16),
             pltpu.VMEM((terms * mb, 4 * mb), jnp.float32),
             pltpu.VMEM((terms * mb, 4 * mb), jnp.float32),
-            pltpu.VMEM((terms * mb, 4 * mb), jnp.bfloat16),
             pltpu.VMEM((terms, 8, ny), jnp.float32),
             pltpu.VMEM((mb, ny), jnp.float32),
             pltpu.VMEM((mb, ny), jnp.float32),
@@ -449,7 +488,7 @@
             pltpu.SemaphoreType.DMA((sides,)),
             pltpu.SemaphoreType.DMA((sides,)),
             pltpu.SemaphoreType.DMA((sides, rows // 2 + 1)),
-            pltpu.SemaphoreType.DMA((sides, 1 + len(LATE))),
+            pltpu.SemaphoreType.DMA((sides, 2)),
             pltpu.SemaphoreType.DMA((5,)),
             pltpu.SemaphoreType.DMA((4,)),
             pltpu.SemaphoreType.DMA((2,)),
@@ -458,6 +497,19 @@
         compiler_params=pltpu.CompilerParams(collective_id=0, has_side_effects=True, vmem_limit_bytes=24 * 2**20),
     )(*[pltpu.with_memory_space_constraint(x, pltpu.HBM)
         for x in (field, kappa_x, kappa_y, coupling, pattern)])
+    handed = [results[0].reshape(mb, across, 128)] + list(results[1:])
+    handed = [pltpu.with_memory_space_constraint(x, pltpu.VMEM) for x in handed]
+    out = pl.pallas_call(
+        functools.partial(closing, rows),
+        out_shape=jax.ShapeDtypeStruct((mb, across, 128), jnp.float32),
+        in_specs=[vmem] * 5,
+        out_specs=hbm,
+        scratch_shapes=[
+            pltpu.VMEM((mb, (width + 128) // 16, 128), jnp.float32),
+            pltpu.SemaphoreType.DMA((2,)),
+        ],
+        compiler_params=pltpu.CompilerParams(vmem_limit_bytes=8 * 2**20),
+    )(*handed)
     tiles = out.reshape(mb, rows // 8, ny // 128, 8, 128)
     return jnp.swapaxes(tiles, 2, 3).reshape(mb, rows, ny)
 

time: 28.6 us -> 28.2 us (0.986)
  local copies, waits for them, and re-layouts: 1.32 us -> 0 us
  Pallas kernels: 27 us -> 28 us
    unnamed x1 -> x0, local copies, waits for them, and re-layouts: 1.32 us -> none
    pallas_call x1 -> x2, Pallas kernels: 27 us -> 28 us  [the longest x1 26.7 us: shards(): pl.pallas_call(functools.partial(kernel, n_mode, n_space), out_shape=[jax...]
where the time goes in v5:
time: 28.2 us; the launch traced here: 28 us
  Pallas kernels  28 us (99%)
    pallas_call x1, Pallas kernels, shards(): pl.pallas_call(functools.partial(kernel, n_mode, n_space), out_shape=[jax...  26.7 us
    pallas_call x1, Pallas kernels, shards(): pl.pallas_call(functools.partial(closing, rows), out_shape=jax.ShapeDtype...  1.34 us

profile of v5, /device:TPU:0, one launch (start us, length us, event | category | flops | bytes accessed | tf_op | source)
XLA Modules:
  0.0 28.0 jit_solution(16533873948596267866)
XLA Ops:
  0.0 26.7 %shard_map.55 = (f32[4096,128]{1,0:T(8,128)S(1)}, bf16[256,128]{1,0:T(8,128)(2,1)S(1)}, bf16[2,32,384]{2,1,0:T(8,128)(2,1)S(1)}, f32[4,32,512]{2,1,0:T(8,128)S(1)}, f32[4,8,384]{2,1,0:T(8,128)S(1)}) custom-call(bf16[32,16,1024]{2,1,0:T(8,128)(2,1)} %field_hbm.1, f32[8,16,1024]{2,1,0:T(8,128)} %kx_hbm.1, f32[8,16,1024]{2,1,0:T(8,128)} %ky_hbm.1, ...), custom_call_target="tpu_custom_call" | custom-call | tf_op jit(solution)/shard_map/pallas_call | solution.py:453
  26.7 1.3 %shard_map.56 = f32[32,128,128]{2,1,0:T(8,128)} custom-call(f32[32,128,128]{2,1,0:T(8,128)S(1)} %bitcast.6, bf16[256,128]{1,0:T(8,128)(2,1)S(1)} %get-tuple-element.11.coef_ref, bf16[2,32,384]{2,1,0:T(8,128)(2,1)S(1)} %get-tuple-element.12.ends_ref, f32[4,32,512]{2,1,0:T(8,128)S(1)} %get-tuple-element.13.rim_ref, f32[4,8,384]{2,1,0:T(8,128)S(1)} %get-tuple-element.14.scale_ref), custom_call_target="tpu_custom_call" | custom-call | tf_op jit(solution)/shard_map/pallas_call | solution.py:502

commit v6 on v5

--- a/solution.py
+++ b/solution.py
@@ -95,7 +95,10 @@
 
     for target in (upper, lower)[:sides]:
         greet(target)
-    pl.when(has_above)(lambda: greet(above))
+    odd = lax.rem(space, 2) == 1
+    pl.when(odd)(lambda: greet(below))
+    pl.when(odd & has_above)(lambda: greet(above))
+    neighbours = jnp.where(has_below, 1, 0) + jnp.where(has_above, 1, 0)
 
     field_load = pltpu.make_async_copy(field_hbm, raw, local_sem.at[0])
     coup_load = pltpu.make_async_copy(coup_hbm, coup, local_sem.at[1])
@@ -120,11 +123,10 @@
             for r in range(count):
                 target[first + r + 1, :, c:c + 128] = tall[pl.ds(r, mb, stride=count), :].astype(jnp.bfloat16)
 
-    pl.semaphore_wait(barrier, sides + jnp.where(has_below, 1, 0))
-
-    @pl.when(has_below)
-    def _():
-        pl.semaphore_signal(hello, inc=1, device_id=below, device_id_type=pl.DeviceIdType.MESH)
+    pl.semaphore_wait(barrier, sides + jnp.where(odd, 0, neighbours))
+
+    def answer(target):
+        pl.semaphore_signal(hello, inc=1, device_id=target, device_id_type=pl.DeviceIdType.MESH)
 
     def remote(src, dst, send, recv, target):
         return pltpu.make_async_remote_copy(
@@ -178,6 +180,8 @@
 
     for side in range(sides):
         early_copy(side).start()
+    pl.when(jnp.logical_not(odd) & has_below)(lambda: answer(below))
+    pl.when(jnp.logical_not(odd) & has_above)(lambda: answer(above))
 
     coup_load.wait()
     pat_load.wait()
@@ -194,12 +198,11 @@
 
     field_load.wait()
     by_rows(raw, u_ext, 0, rows, ny)
-    pl.when(has_above)(lambda: pl.semaphore_wait(hello, 1))
+    pl.when(odd)(lambda: pl.semaphore_wait(hello, neighbours))
 
     detours = [(1, ny - early), (3, min(ASIDE, ny - early))] if sides == 1 and n_space > 4 else []
-    strong = (mode == 1) & ((space == 1) | (space == 3))
-    weak = (mode == 1) & (lax.rem(space, 2) == 1) & (space > 3)
-    yields = strong | weak if detours else space < 0
+    weak = odd
+    yields = weak if detours else space < 0
     hops = []
     for at, width in detours:
         part = pl.ds(early, width)
@@ -231,16 +234,12 @@
             cross_copy.start()
     for side in range(sides):
         rows_copy(side, rows - 1, 1, 1).start()
-    early_rows(jnp.logical_not(strong))
-    for _, _, turn, _, cross_copy, come_copy in hops:
-        @pl.when(turn)
-        def _():
-            cross_copy.wait_recv()
-            come_copy.start()
+    early_rows(space >= 0)
+    turns = space < 0
+    for hop in hops:
+        turns = turns | hop[2]
 
     def send_rest():
-        if detours:
-            early_rows(strong)
         for side in range(sides):
             @pl.loop(0, pairs)
             def _(h):
@@ -256,7 +255,7 @@
             last_copy.start()
             kx_copy.start()
 
-    pl.when(jnp.logical_not(yields))(send_rest)
+    pl.when(jnp.logical_not(yields | turns))(send_rest)
 
     for k in range(terms):
         half = masked(0, k) * 0.5
@@ -287,8 +286,13 @@
     for side in range(sides):
         rows_copy(side, 0, 2, 0).wait_recv()
         pl.when(has_below)(halo_down(side).start)
+    for _, _, turn, _, cross_copy, come_copy in hops:
+        @pl.when(turn)
+        def _():
+            cross_copy.wait_recv()
+            come_copy.start()
     if detours:
-        pl.when(yields)(send_rest)
+        pl.when(yields | turns)(send_rest)
     for side in range(sides):
         rows_copy(side, rows - 1, 1, 1).wait_recv()
         pl.when(has_above)(halo_up(side).start)

time: 28.2 us -> 27.9 us (0.989); the launches traced: 28 us -> 27.4 us
  Pallas kernels: 28 us -> 27.4 us
    pallas_call x1, Pallas kernels: 26.7 us -> 26 us  [shards(): pl.pallas_call(functools.partial(kernel, n_mode, n_space), out_shape=[jax...]
where the time goes in v6:
time: 27.9 us; the launch traced here: 27.4 us
  Pallas kernels  27.4 us (98%)
    pallas_call x1, Pallas kernels, shards(): pl.pallas_call(functools.partial(kernel, n_mode, n_space), out_shape=[jax...  26 us
    pallas_call x1, Pallas kernels, shards(): pl.pallas_call(functools.partial(closing, rows), out_shape=jax.ShapeDtype...  1.34 us

profile of v6, /device:TPU:0, one launch (start us, length us, event | category | flops | bytes accessed | tf_op | source)
XLA Modules:
  0.0 27.4 jit_solution(11354915286081134279)
XLA Ops:
  0.0 26.0 %shard_map.55 = (f32[4096,128]{1,0:T(8,128)S(1)}, bf16[256,128]{1,0:T(8,128)(2,1)S(1)}, bf16[2,32,384]{2,1,0:T(8,128)(2,1)S(1)}, f32[4,32,512]{2,1,0:T(8,128)S(1)}, f32[4,8,384]{2,1,0:T(8,128)S(1)}) custom-call(bf16[32,16,1024]{2,1,0:T(8,128)(2,1)} %field_hbm.1, f32[8,16,1024]{2,1,0:T(8,128)} %kx_hbm.1, f32[8,16,1024]{2,1,0:T(8,128)} %ky_hbm.1, ...), custom_call_target="tpu_custom_call" | custom-call | tf_op jit(solution)/shard_map/pallas_call | solution.py:457
  26.0 1.3 %shard_map.56 = f32[32,128,128]{2,1,0:T(8,128)} custom-call(f32[32,128,128]{2,1,0:T(8,128)S(1)} %bitcast.6, bf16[256,128]{1,0:T(8,128)(2,1)S(1)} %get-tuple-element.11.coef_ref, bf16[2,32,384]{2,1,0:T(8,128)(2,1)S(1)} %get-tuple-element.12.ends_ref, f32[4,32,512]{2,1,0:T(8,128)S(1)} %get-tuple-element.13.rim_ref, f32[4,8,384]{2,1,0:T(8,128)S(1)} %get-tuple-element.14.scale_ref), custom_call_target="tpu_custom_call" | custom-call | tf_op jit(solution)/shard_map/pallas_call | solution.py:506

commit v7 on v6

--- a/solution.py
+++ b/solution.py
@@ -203,6 +203,7 @@
     detours = [(1, ny - early), (3, min(ASIDE, ny - early))] if sides == 1 and n_space > 4 else []
     weak = odd
     yields = weak if detours else space < 0
+    late_yield = odd & (mode == 0) if detours else space < 0
     hops = []
     for at, width in detours:
         part = pl.ds(early, width)
@@ -234,14 +235,19 @@
             cross_copy.start()
     for side in range(sides):
         rows_copy(side, rows - 1, 1, 1).start()
-    early_rows(space >= 0)
+    early_rows(jnp.logical_not(late_yield))
     turns = space < 0
     for hop in hops:
         turns = turns | hop[2]
 
+    if detours:
+        pl.when(turns)(pair_copy(0, 0).start)
+
     def send_rest():
+        if detours:
+            early_rows(late_yield)
         for side in range(sides):
-            @pl.loop(0, pairs)
+            @pl.loop(jnp.where(turns, 1, 0), pairs)
             def _(h):
                 pair_copy(side, h).start()
         for side in range(sides):

time: 27.9 us -> 27.8 us (level)
  no operation moved by 1% of the time
where the time goes in v7:
time: 27.8 us; the launch traced here: 27.4 us
  Pallas kernels  27.4 us (99%)
    pallas_call x1, Pallas kernels, shards(): pl.pallas_call(functools.partial(kernel, n_mode, n_space), out_shape=[jax...  26 us
    pallas_call x1, Pallas kernels, shards(): pl.pallas_call(functools.partial(closing, rows), out_shape=jax.ShapeDtype...  1.34 us

profile of v7, /device:TPU:0, one launch (start us, length us, event | category | flops | bytes accessed | tf_op | source)
XLA Modules:
  0.0 27.4 jit_solution(10742328335624265274)
XLA Ops:
  0.0 26.0 %shard_map.55 = (f32[4096,128]{1,0:T(8,128)S(1)}, bf16[256,128]{1,0:T(8,128)(2,1)S(1)}, bf16[2,32,384]{2,1,0:T(8,128)(2,1)S(1)}, f32[4,32,512]{2,1,0:T(8,128)S(1)}, f32[4,8,384]{2,1,0:T(8,128)S(1)}) custom-call(bf16[32,16,1024]{2,1,0:T(8,128)(2,1)} %field_hbm.1, f32[8,16,1024]{2,1,0:T(8,128)} %kx_hbm.1, f32[8,16,1024]{2,1,0:T(8,128)} %ky_hbm.1, ...), custom_call_target="tpu_custom_call" | custom-call | tf_op jit(solution)/shard_map/pallas_call | solution.py:463
  26.0 1.3 %shard_map.56 = f32[32,128,128]{2,1,0:T(8,128)} custom-call(f32[32,128,128]{2,1,0:T(8,128)S(1)} %bitcast.6, bf16[256,128]{1,0:T(8,128)(2,1)S(1)} %get-tuple-element.11.coef_ref, bf16[2,32,384]{2,1,0:T(8,128)(2,1)S(1)} %get-tuple-element.12.ends_ref, f32[4,32,512]{2,1,0:T(8,128)S(1)} %get-tuple-element.13.rim_ref, f32[4,8,384]{2,1,0:T(8,128)S(1)} %get-tuple-element.14.scale_ref), custom_call_target="tpu_custom_call" | custom-call | tf_op jit(solution)/shard_map/pallas_call | solution.py:512

commit v8 on v7

--- a/solution.py
+++ b/solution.py
@@ -168,11 +168,12 @@
 
     shared = n_space % 2 == 0
     sends_coup = lax.rem(space, 2) == 0 if shared else space >= 0
-    coup_pass = remote(packed_in, packed_in, other_send.at[4], other_recv.at[0], above)
+    coup_pass = remote(packed_in, packed_in, other_send.at[3], other_recv.at[0], above)
     coup_copy = remote(packed, packed_in, other_send.at[0], other_recv.at[0], upper)
     last_copy = remote(u_ext.at[rows], u_ext.at[0], other_send.at[1], other_recv.at[1], above)
     first_copy = remote(u_ext.at[1], u_ext.at[rows + 1], other_send.at[2], other_recv.at[2], below)
-    kx_copy = remote(kx_hbm.at[:, pl.ds(rows - 8, 8), :], kx_in, other_send.at[3], other_recv.at[3], above)
+    kx_copy = remote(kx_hbm.at[:, pl.ds(rows - 8, 8), :], kx_in, other_send.at[1], other_recv.at[1], above)
+    upward = 1 + sides + terms * 16 // mb
 
     def strips(count, sem):
         part = u_ext.at[pl.ds(0, count)]
@@ -343,8 +344,7 @@
     def edges():
         @pl.when(has_below)
         def _():
-            strips(1 + sides, other_recv.at[1]).wait()
-            kx_copy.wait_recv()
+            strips(upward, other_recv.at[1]).wait()
 
         @pl.when(has_above)
         def _():
@@ -444,8 +444,7 @@
 
     @pl.when(has_above)
     def _():
-        strips(1 + sides, other_send.at[1]).wait()
-        kx_copy.wait_send()
+        strips(upward, other_send.at[1]).wait()
 
     @pl.when(has_below)
     def _():
@@ -499,8 +498,8 @@
             pltpu.SemaphoreType.DMA((sides,)),
             pltpu.SemaphoreType.DMA((sides, rows // 2 + 1)),
             pltpu.SemaphoreType.DMA((sides, 2)),
-            pltpu.SemaphoreType.DMA((5,)),
             pltpu.SemaphoreType.DMA((4,)),
+            pltpu.SemaphoreType.DMA((3,)),
             pltpu.SemaphoreType.DMA((2,)),
             pltpu.SemaphoreType.REGULAR,
         ],

time: 27.8 us -> 27.8 us (level)
  no operation moved by 1% of the time
where the time goes in v8:
time: 27.8 us; the launch traced here: 27.4 us
  Pallas kernels  27.4 us (99%)
    pallas_call x1, Pallas kernels, shards(): pl.pallas_call(functools.partial(kernel, n_mode, n_space), out_shape=[jax...  26 us
    pallas_call x1, Pallas kernels, shards(): pl.pallas_call(functools.partial(closing, rows), out_shape=jax.ShapeDtype...  1.34 us

profile of v8, /device:TPU:0, one launch (start us, length us, event | category | flops | bytes accessed | tf_op | source)
XLA Modules:
  0.0 27.4 jit_solution(11638554922334686220)
XLA Ops:
  0.0 26.0 %shard_map.55 = (f32[4096,128]{1,0:T(8,128)S(1)}, bf16[256,128]{1,0:T(8,128)(2,1)S(1)}, bf16[2,32,384]{2,1,0:T(8,128)(2,1)S(1)}, f32[4,32,512]{2,1,0:T(8,128)S(1)}, f32[4,8,384]{2,1,0:T(8,128)S(1)}) custom-call(bf16[32,16,1024]{2,1,0:T(8,128)(2,1)} %field_hbm.1, f32[8,16,1024]{2,1,0:T(8,128)} %kx_hbm.1, f32[8,16,1024]{2,1,0:T(8,128)} %ky_hbm.1, ...), custom_call_target="tpu_custom_call" | custom-call | tf_op jit(solution)/shard_map/pallas_call | solution.py:462
  26.0 1.3 %shard_map.56 = f32[32,128,128]{2,1,0:T(8,128)} custom-call(f32[32,128,128]{2,1,0:T(8,128)S(1)} %bitcast.6, bf16[256,128]{1,0:T(8,128)(2,1)S(1)} %get-tuple-element.11.coef_ref, bf16[2,32,384]{2,1,0:T(8,128)(2,1)S(1)} %get-tuple-element.12.ends_ref, f32[4,32,512]{2,1,0:T(8,128)S(1)} %get-tuple-element.13.rim_ref, f32[4,8,384]{2,1,0:T(8,128)S(1)} %get-tuple-element.14.scale_ref), custom_call_target="tpu_custom_call" | custom-call | tf_op jit(solution)/shard_map/pallas_call | solution.py:511

commit v9 on v8

--- a/solution.py
+++ b/solution.py
@@ -241,8 +241,10 @@
     for hop in hops:
         turns = turns | hop[2]
 
+    first_source = hops[0][0] if hops else space < 0
     if detours:
         pl.when(turns)(pair_copy(0, 0).start)
+        pl.when(first_source)(late_row(0).start)
 
     def send_rest():
         if detours:
@@ -252,7 +254,7 @@
             def _(h):
                 pair_copy(side, h).start()
         for side in range(sides):
-            late_row(side).start()
+            pl.when(jnp.logical_not(first_source))(late_row(side).start)
         for p in range(len(pieces)):
             for side in range(sides):
                 piece_copy(side, p).start()

time: 27.8 us -> 28 us (level); the launches traced: 27.4 us -> 27.9 us
  Pallas kernels: 27.4 us -> 27.9 us
    pallas_call x1, Pallas kernels: 26 us -> 26.5 us  [shards(): pl.pallas_call(functools.partial(kernel, n_mode, n_space), out_shape=[jax...]
where the time goes in v9:
time: 28 us; the launch traced here: 27.9 us
  Pallas kernels  27.9 us (100%)
    pallas_call x1, Pallas kernels, shards(): pl.pallas_call(functools.partial(kernel, n_mode, n_space), out_shape=[jax...  26.5 us
    pallas_call x1, Pallas kernels, shards(): pl.pallas_call(functools.partial(closing, rows), out_shape=jax.ShapeDtype...  1.34 us

profile of v9, /device:TPU:0, one launch (start us, length us, event | category | flops | bytes accessed | tf_op | source)
XLA Modules:
  0.0 27.9 jit_solution(3656880774556715501)
XLA Ops:
  0.0 26.5 %shard_map.55 = (f32[4096,128]{1,0:T(8,128)S(1)}, bf16[256,128]{1,0:T(8,128)(2,1)S(1)}, bf16[2,32,384]{2,1,0:T(8,128)(2,1)S(1)}, f32[4,32,512]{2,1,0:T(8,128)S(1)}, f32[4,8,384]{2,1,0:T(8,128)S(1)}) custom-call(bf16[32,16,1024]{2,1,0:T(8,128)(2,1)} %field_hbm.1, f32[8,16,1024]{2,1,0:T(8,128)} %kx_hbm.1, f32[8,16,1024]{2,1,0:T(8,128)} %ky_hbm.1, ...), custom_call_target="tpu_custom_call" | custom-call | tf_op jit(solution)/shard_map/pallas_call | solution.py:464
  26.5 1.3 %shard_map.56 = f32[32,128,128]{2,1,0:T(8,128)} custom-call(f32[32,128,128]{2,1,0:T(8,128)S(1)} %bitcast.6, bf16[256,128]{1,0:T(8,128)(2,1)S(1)} %get-tuple-element.11.coef_ref, bf16[2,32,384]{2,1,0:T(8,128)(2,1)S(1)} %get-tuple-element.12.ends_ref, f32[4,32,512]{2,1,0:T(8,128)S(1)} %get-tuple-element.13.rim_ref, f32[4,8,384]{2,1,0:T(8,128)S(1)} %get-tuple-element.14.scale_ref), custom_call_target="tpu_custom_call" | custom-call | tf_op jit(solution)/shard_map/pallas_call | solution.py:513
